TPU v7x, 32 devices: a whole 2x2x4 slice. The times are simulated.
32 devices in a mesh: dp: 8 (over z, y), tensor: 4 (over x, core).
Axes of the slice: x: 2, y: 2, z: 4, core: 2. Of those that a mesh axis runs over, the one named last changes fastest.
Arguments:
- tokens: bfloat16 [3, 4096, 1536], P(None, ('dp', 'tensor')), may hold values from -6 to 6
- lengths: int32 [3, 32, 6], P(None, ('dp', 'tensor')), may hold values from 1 to 64, 128 in all within a row
- first_gain: bfloat16 [1536], P(('dp', 'tensor')), may hold values from 0.099609375 to 1.8984375
- query_weight: bfloat16 [1536, 1536], P(('dp', 'tensor')), may hold values from -0.15625 to 0.15625
- key_weight: bfloat16 [1536, 768], P(('dp', 'tensor')), may hold values from -0.15625 to 0.15625
- value_weight: bfloat16 [1536, 768], P(('dp', 'tensor')), may hold values from -0.15625 to 0.15625
- output_weight: bfloat16 [1536, 1536], P(('dp', 'tensor')), may hold values from -0.4375 to 0.4375
- second_gain: bfloat16 [1536], P(('dp', 'tensor')), may hold values from 0.099609375 to 1.8984375
- gate_weight: bfloat16 [1536, 4096], P('dp', 'tensor'), may hold values from -0.15625 to 0.15625
- up_weight: bfloat16 [1536, 4096], P('dp', 'tensor'), may hold values from -0.15625 to 0.15625
- down_weight: bfloat16 [4096, 1536], P('tensor', 'dp'), may hold values from -0.09375 to 0.09375
- cotangent: bfloat16 [3, 4096, 1536], P(None, ('dp', 'tensor')), may hold values from -6 to 6
Outputs:
- layer_out: bfloat16 [3, 4096, 1536], P(None, ('dp', 'tensor'))
- input_grad: float32 [3, 4096, 1536], P(None, ('dp', 'tensor'))
- first_gain_grad: float32 [1536], P(('dp', 'tensor'))
- query_grad: float32 [1536, 1536], P(('dp', 'tensor'))
- key_grad: float32 [1536, 768], P(('dp', 'tensor'))
- value_grad: float32 [1536, 768], P(('dp', 'tensor'))
- output_grad: float32 [1536, 1536], P(('dp', 'tensor'))
- second_gain_grad: float32 [1536], P(('dp', 'tensor'))
- gate_grad: float32 [1536, 4096], P('dp', 'tensor')
- up_grad: float32 [1536, 4096], P('dp', 'tensor')
- down_grad: float32 [4096, 1536], P('tensor', 'dp')
Inputs may be any that keep to these rules, and one draw needn't show every extreme that they name: Row lengths[m, p] splits the 128 rows of pack p of micro-batch m into 6 runs in order, summing to 128; the first 5 runs are sequences, the last is padding; no run is longer than 64 rows.
All inputs are finite; a program needn't handle non-finite values.
Results may differ from a plain program's by a relative error of at most 0.013.
Values may be sent and summed in bfloat16 or wider, within the bound.
No kernel may reach another device: no remote copies, remote signals or barrier semaphores. Data moves between devices by JAX's collectives and lax.ppermute only.
A program may use at most 192 MiB of HBM per device.

v0:
```python
import math
import jax
import jax.numpy as jnp
from jax import lax
from jax.sharding import PartitionSpec as P

HEADS = 16
KV_HEADS = 8
HEAD = 96
SLOTS = 6
GROUP = HEADS // KV_HEADS
LANES = 128
EPSILON = 1e-05
ROPE_BASE = 100000.0
NEG_LARGE = -1e30
AXES = ("dp", "tensor")
bf16 = jnp.bfloat16
f32 = jnp.float32


def pack_layout(seq_lengths, row_count):
    seq_ends = jnp.cumsum(seq_lengths)
    seq_starts = seq_ends - seq_lengths
    row_index = jnp.arange(row_count, dtype=jnp.int32)
    segment = jnp.sum((row_index[:, None] >= seq_ends[None, :]).astype(jnp.int32), axis=1)
    owner_hot = segment[:, None] == jnp.arange(seq_lengths.shape[0], dtype=jnp.int32)[None, :]
    position = row_index - jnp.sum(jnp.where(owner_hot, seq_starts[None, :], 0), axis=1)
    return (segment, position)


def rotary_tables(position, head_size):
    half_size = head_size // 2
    freq_index = jnp.arange(half_size, dtype=f32)
    inverse = jnp.exp(freq_index * (-2.0 / head_size) * math.log(ROPE_BASE))
    angles = position.astype(f32)[..., None] * inverse
    return (jnp.cos(angles), jnp.sin(angles))


def rotate(vectors, cosine, sine_part):
    half_size = vectors.shape[-1] // 2
    lower_half = vectors[..., :half_size]
    upper_half = vectors[..., half_size:]
    cosine = cosine[..., None, :]
    sine_part = sine_part[..., None, :]
    return jnp.concatenate(
        [
            lower_half * cosine - upper_half * sine_part,
            upper_half * cosine + lower_half * sine_part,
        ],
        axis=-1,
    )


def product(left_side, right_side):
    return jnp.dot(left_side, right_side, preferred_element_type=f32)


def across(left_side, right_side):
    return lax.dot_general(
        left_side, right_side, (((0,), (0,)), ((), ())), preferred_element_type=f32
    )


def against(left_side, right_side):
    return lax.dot_general(
        left_side, right_side, (((1,), (1,)), ((), ())), preferred_element_type=f32
    )


def bits_of(size):
    return [1 << k for k in range(size.bit_length() - 1)]


def near_first(size):
    masks = bits_of(size)
    return masks[:1] + masks[:0:-1]


def far_first(size):
    return bits_of(size)[::-1]


def rel_source(me, masks, block, count):
    place = jnp.arange(count, dtype=jnp.int32)
    step = place // block
    delta = jnp.zeros_like(step)
    for k, mask in enumerate(masks):
        delta = delta + (step >> k & 1) * mask
    return (me ^ delta) * block + place % block


def one_hot(source):
    count = source.shape[0]
    rows = lax.broadcasted_iota(jnp.int32, (count, count), 0)
    return (rows == source[None, :]).astype(bf16)


def join(parts):
    return parts[0] if len(parts) == 1 else jnp.concatenate(parts, axis=0)


def program(sizes):
    dp_n, tp_n = (sizes["dp"], sizes["tensor"])
    world = dp_n * tp_n

    def swap(array, mask):
        return lax.ppermute(array, AXES, [(i, i ^ mask) for i in range(world)])

    def gather(own, masks, loose):
        held = [own]
        for k, mask in enumerate(masks):
            got = [swap(part, mask) for part in held]
            held = held + got
            if k < len(masks) - loose:
                held = [join(held)]
        return held

    def per_device(
        tokens,
        lengths,
        first_gain,
        query_weight,
        key_weight,
        value_weight,
        output_weight,
        second_gain,
        gate_weight,
        up_weight,
        down_weight,
        cotangent,
    ):
        micro, per_pack, width = tokens.shape
        rows = micro * per_pack
        qw, kw = (query_weight.shape[1], key_weight.shape[1])
        ff = gate_weight.shape[1]
        wide = qw + 2 * kw
        shard = query_weight.shape[0]
        dp_i, t_i = (lax.axis_index("dp"), lax.axis_index("tensor"))
        me = dp_i * tp_n + t_i
        dp_attn = [m * tp_n for m in near_first(dp_n)]
        t_bits = bits_of(tp_n)[::-1]
        attn_masks = dp_attn + t_bits
        mlp_masks = [m * tp_n for m in far_first(dp_n)]
        x_low = tokens.reshape(rows, width)
        dy_low = cotangent.reshape(rows, width)
        gains = jnp.pad(jnp.stack([first_gain, second_gain], axis=1), ((0, 0), (0, LANES - 2)))
        own_qkv = jnp.concatenate([query_weight, key_weight, value_weight, gains], axis=1)
        own_gu = jnp.concatenate([gate_weight, up_weight], axis=1)
        own_down = down_weight.T

        def gather_attn(own):
            held = gather(own, dp_attn, 2)
            far = [swap(part, t_bits[0]) for part in held]
            pieces = [join(held), join(far)]
            for mask in t_bits[1:]:
                pieces = pieces + [swap(part, mask) for part in pieces]
            return pieces

        qkv_pieces = gather_attn(own_qkv)
        out_pieces = gather_attn(output_weight)
        gu_full = join(gather(own_gu, mlp_masks, 3))
        down_full = join(gather(own_down, mlp_masks, 3))
        n_pieces = len(qkv_pieces)
        part = width // n_pieces
        pick_attn = one_hot(rel_source(me, attn_masks, shard, width))
        mlp_source = rel_source(dp_i, [m // tp_n for m in mlp_masks], shard * tp_n, width)
        pick_mlp = one_hot(mlp_source)

        def order(array, pick):
            return product(array, pick).astype(bf16)

        def restore(array, pick):
            return against(array, pick)

        gains_rel = jnp.concatenate([piece[:, wide : wide + 2] for piece in qkv_pieces], axis=0)
        g1_rel = gains_rel[:, 0].astype(f32)
        g2 = restore(gains_rel[:, 1][None, :], pick_attn)[0]
        segment, position = jax.vmap(lambda own: pack_layout(own, per_pack))(lengths[:, 0])
        cosine, sine_part = rotary_tables(position, HEAD)
        row_index = jnp.arange(per_pack, dtype=jnp.int32)
        allowed = (
            (segment[:, :, None] == segment[:, None, :])
            & (row_index[None, None, :] <= row_index[None, :, None])
            & (segment < SLOTS - 1)[:, :, None]
        )[:, None, None]
        factor = 1.0 / math.sqrt(HEAD)
        inputs = x_low.astype(f32)
        r1 = lax.rsqrt(jnp.mean(inputs * inputs, axis=1, keepdims=True) + EPSILON)
        x_rel = order(x_low, pick_attn).astype(f32)
        n1_rel = (x_rel * r1 * g1_rel).astype(bf16)
        n1_parts = [n1_rel[:, k * part : (k + 1) * part] for k in range(n_pieces)]
        qkv = sum((product(a, b) for a, b in zip(n1_parts, qkv_pieces)))
        shape = (micro, per_pack)
        queries = rotate(qkv[:, :qw].reshape(shape + (HEADS, HEAD)), cosine, sine_part)
        queries = queries.astype(bf16).reshape(shape + (KV_HEADS, GROUP, HEAD))
        keys = rotate(
            qkv[:, qw : qw + kw].reshape(shape + (KV_HEADS, HEAD)), cosine, sine_part
        ).astype(bf16)
        values = qkv[:, qw + kw : wide].astype(bf16).reshape(shape + (KV_HEADS, HEAD))
        scores = jnp.einsum("pqhgd,pkhd->phgqk", queries, keys, preferred_element_type=f32) * factor
        row_peak = jnp.max(jnp.where(allowed, scores, NEG_LARGE), axis=-1, keepdims=True)
        raised = jnp.where(allowed, jnp.exp(jnp.where(allowed, scores - row_peak, 0.0)), 0.0)
        totals = jnp.sum(raised, axis=-1, keepdims=True)
        probs = raised / jnp.where(totals > 0, totals, 1.0)
        probs_low = probs.astype(bf16)
        attended = jnp.einsum("phgqk,pkhd->pqhgd", probs_low, values, preferred_element_type=f32)
        attended = attended.reshape(rows, qw).astype(bf16)
        att_rel = order(attended, pick_attn)
        att_parts = [att_rel[:, k * part : (k + 1) * part] for k in range(n_pieces)]
        middle = inputs + sum((product(a, b) for a, b in zip(att_parts, out_pieces)))
        r2 = lax.rsqrt(jnp.mean(middle * middle, axis=1, keepdims=True) + EPSILON)
        n2 = (middle * r2 * g2).astype(bf16)
        n2_rel = order(n2, pick_mlp)
        dy_rel = order(dy_low, pick_mlp)

        def spread(own):
            return join(gather(own, t_bits, tp_n))

        def collect(partial):
            for mask in t_bits[::-1]:
                half = partial.shape[0] // 2
                got = swap(partial[half:].astype(bf16), mask)
                partial = partial[:half].astype(f32) + got.astype(f32)
            return partial

        dy_all = spread(dy_rel)
        n2_all = spread(n2_rel)
        gu = product(n2_all, gu_full)
        gate, up = (gu[:, :ff], gu[:, ff:])
        sig = jax.nn.sigmoid(gate)
        hidden = (gate * sig * up).astype(bf16)
        dhid = product(dy_all, down_full)
        dgate = (dhid * up * sig * (1.0 + gate * (1.0 - sig))).astype(bf16)
        dup = (dhid * gate * sig).astype(bf16)
        dgu = jnp.concatenate([dgate, dup], axis=1)
        dn2 = restore(collect(against(dgu, gu_full).astype(bf16)).astype(bf16), pick_mlp)
        down_sum = collect(against(hidden, down_full).astype(bf16)).astype(bf16)
        layer_out = (middle + restore(down_sum, pick_mlp)).astype(bf16)

        def reduce_rows(own_half, sent_half, masks):
            total = own_half() + swap(sent_half().astype(bf16), masks[0]).astype(f32)
            for mask in masks[1:]:
                half = total.shape[0] // 2
                got = swap(total[half:].astype(bf16), mask)
                total = total[:half] + got.astype(f32)
            return total

        half = width // 2

        def mlp_grad(left, right):
            return reduce_rows(
                lambda: across(left[:, :half], right),
                lambda: across(left[:, half:], right),
                mlp_masks[::-1],
            )

        down_grad = mlp_grad(dy_all, hidden).T
        gate_grad = mlp_grad(n2_all, dgate)
        up_grad = mlp_grad(n2_all, dup)
        dy = dy_low.astype(f32)
        weighted = dn2 * g2
        dmid = (
            dy
            + r2 * weighted
            - middle * (r2 * r2 * r2) * jnp.mean(weighted * middle, axis=1, keepdims=True)
        )
        dmb = dmid.astype(bf16)

        def attn_grad(lefts, right):
            held = [across(left, right) for left in lefts]
            for mask in t_bits[1:][::-1]:
                n = len(held) // 2
                got = [swap(piece.astype(bf16), mask) for piece in held[n:]]
                held = [a + b.astype(f32) for a, b in zip(held[:n], got)]
            return reduce_rows(lambda: held[0], lambda: held[1], [t_bits[0]] + dp_attn[::-1])

        output_grad = attn_grad(att_parts, dmb)
        datt_rel = jnp.concatenate([against(dmb, piece) for piece in out_pieces], axis=1)
        datt = restore(datt_rel.astype(bf16), pick_attn).astype(bf16)
        datt = datt.reshape(shape + (KV_HEADS, GROUP, HEAD))
        dprob = jnp.einsum("pqhgd,pkhd->phgqk", datt, values, preferred_element_type=f32)
        delta = jnp.sum(probs * dprob, axis=-1, keepdims=True)
        dscore = (probs * (dprob - delta)).astype(bf16)
        dvalue = jnp.einsum("phgqk,pqhgd->pkhd", probs_low, datt, preferred_element_type=f32)
        dqr = jnp.einsum("phgqk,pkhd->pqhgd", dscore, keys, preferred_element_type=f32) * factor
        dkr = jnp.einsum("phgqk,pqhgd->pkhd", dscore, queries, preferred_element_type=f32) * factor
        dq = rotate(dqr.reshape(shape + (HEADS, HEAD)), cosine, -sine_part)
        dk = rotate(dkr, cosine, -sine_part)
        dqkv = jnp.concatenate(
            [
                dq.astype(bf16).reshape(rows, qw),
                dk.astype(bf16).reshape(rows, kw),
                dvalue.astype(bf16).reshape(rows, kw),
            ],
            axis=1,
        )
        qkv_grad = attn_grad(n1_parts, dqkv)
        dn1_rel = jnp.concatenate([against(dqkv, piece[:, :wide]) for piece in qkv_pieces], axis=1)
        weighted = dn1_rel * g1_rel
        part_rel = r1 * weighted - x_rel * (r1 * r1 * r1) * jnp.mean(
            weighted * x_rel, axis=1, keepdims=True
        )
        high = part_rel.astype(bf16)
        low = (part_rel - high.astype(f32)).astype(bf16)
        input_grad = dmid + restore(high, pick_attn) + restore(low, pick_attn)
        own_wide = own_qkv[:, :wide].astype(f32)
        first_gain_grad = jnp.sum(own_wide * qkv_grad, axis=1) / first_gain.astype(f32)
        second = jnp.sum(
            gate_weight.astype(f32) * gate_grad + up_weight.astype(f32) * up_grad, axis=1
        )
        second = lax.psum(second, "tensor")
        second = lax.dynamic_slice(second, (t_i * shard,), (shard,))
        second_gain_grad = second / second_gain.astype(f32)
        return (
            layer_out.reshape(tokens.shape),
            input_grad.reshape(tokens.shape),
            first_gain_grad,
            qkv_grad[:, :qw],
            qkv_grad[:, qw : qw + kw],
            qkv_grad[:, qw + kw :],
            output_grad,
            second_gain_grad,
            gate_grad,
            up_grad,
            down_grad,
        )

    return per_device


def solution(mesh):
    rows = P(None, AXES, None)
    split = P(AXES, None)
    placed = (
        rows,
        rows,
        P(AXES),
        split,
        split,
        split,
        split,
        P(AXES),
        P("dp", "tensor"),
        P("dp", "tensor"),
        P("tensor", "dp"),
        rows,
    )
    return jax.shard_map(
        program(dict(mesh.shape)),
        mesh=mesh,
        in_specs=placed,
        out_specs=(
            rows,
            rows,
            P(AXES),
            split,
            split,
            split,
            split,
            P(AXES),
            P("dp", "tensor"),
            P("dp", "tensor"),
            P("tensor", "dp"),
        ),
        check_vma=False,
    )
```

profile of v0, /device:TPU:0, one launch (start us, length us, event | category | flops | bytes accessed | tf_op | source)
XLA Modules:
  0.0 805.7 jit_solution(15397457779507763800)
XLA Ops:
  0.7 4.1 collective-permute-start.30
  19.4 3.3 fusion.57
  29.8 8.6 %collective-permute-done.4 = bf16[96,3200]{1,0:T(8,128)(2,1)S(1)} collective-permute-done((bf16[96,3200]{1,0:T(8,128)(2,1)S(1)}, bf16[96,3200]{1,0:T(8,128)(2,1)S(1)}, u32[]{:S(2)}, u32[]{:S(2)}) %collective-permute-start.4) | collective-permute-done | bytes 614432 | tf_op jit(solution)/shard_map/ppermute | solution.py:107
  39.7 27.5 %collective-permute-done.1 = bf16[96,3200]{1,0:T(8,128)(2,1)S(1)} collective-permute-done((bf16[96,3200]{1,0:T(8,128)(2,1)S(1)}, bf16[96,3200]{1,0:T(8,128)(2,1)S(1)}, u32[]{:S(2)}, u32[]{:S(2)}) %collective-permute-start.1) | collective-permute-done | bytes 614432 | tf_op jit(solution)/shard_map/ppermute | solution.py:107
  68.1 4.7 collective-permute-done.2
  76.1 8.4 %collective-permute-done.3 = bf16[96,3200]{1,0:T(8,128)(2,1)S(1)} collective-permute-done((bf16[96,3200]{1,0:T(8,128)(2,1)S(1)}, bf16[96,3200]{1,0:T(8,128)(2,1)S(1)}, u32[]{:S(2)}, u32[]{:S(2)}) %collective-permute-start.3) | collective-permute-done | bytes 614432 | tf_op jit(solution)/shard_map/ppermute | solution.py:107
  88.3 13.0 %collective-permute-done.6 = bf16[96,3200]{1,0:T(8,128)(2,1)S(1)} collective-permute-done((bf16[96,3200]{1,0:T(8,128)(2,1)S(1)}, bf16[96,3200]{1,0:T(8,128)(2,1)S(1)}, u32[]{:S(2)}, u32[]{:S(2)}) %collective-permute-start.6) | collective-permute-done | bytes 614432 | tf_op jit(solution)/shard_map/ppermute | solution.py:107
  102.2 9.9 %collective-permute-done.7 = bf16[96,3200]{1,0:T(8,128)(2,1)S(1)} collective-permute-done((bf16[96,3200]{1,0:T(8,128)(2,1)S(1)}, bf16[96,3200]{1,0:T(8,128)(2,1)S(1)}, u32[]{:S(2)}, u32[]{:S(2)}) %collective-permute-start.7) | collective-permute-done | bytes 614432 | tf_op jit(solution)/shard_map/ppermute | solution.py:107
  119.2 5.5 collective-permute-done.14
  126.7 4.3 collective-permute-done.15
  132.5 3.8 collective-permute-done.16
  141.3 7.3 collective-permute-done.34
  149.2 23.1 %collective-permute-done.23 = bf16[192,2048]{1,0:T(8,128)(2,1)S(1)} collective-permute-done((bf16[192,2048]{1,0:T(8,128)(2,1)}, bf16[192,2048]{1,0:T(8,128)(2,1)S(1)}, u32[]{:S(2)}, u32[]{:S(2)}) %collective-permute-start.23) | collective-permute-done | bytes 786464 | tf_op jit(solution)/shard_map/ppermute | solution.py:107
  180.7 4.3 multiply_convert_fusion.4
  185.1 3.6 fusion.149
  188.7 3.7 fusion.137
  192.4 3.2 fusion.140
  195.6 3.4 fusion.15
  208.1 2.9 reshape.243
  211.0 3.7 subtract_convert_fusion.1
  220.8 2.8 fusion.181
  254.1 18.8 %collective-permute-done.36 = bf16[192,1024]{1,0:T(8,128)(2,1)S(1)} collective-permute-done((bf16[192,1024]{1,0:T(8,128)(2,1)S(1)}, bf16[192,1024]{1,0:T(8,128)(2,1)S(1)}, u32[]{:S(2)}, u32[]{:S(2)}) %collective-permute-start.36) | collective-permute-done | bytes 393248 | tf_op jit(solution)/shard_map/ppermute | solution.py:107
  280.2 13.4 %collective-permute-done.28 = bf16[192,2048]{1,0:T(8,128)(2,1)S(1)} collective-permute-done((bf16[192,2048]{1,0:T(8,128)(2,1)}, bf16[192,2048]{1,0:T(8,128)(2,1)S(1)}, u32[]{:S(2)}, u32[]{:S(2)}) %collective-permute-start.28) | collective-permute-done | bytes 786464 | tf_op jit(solution)/shard_map/ppermute | solution.py:107
  295.1 13.2 %collective-permute-done.29 = bf16[192,2048]{1,0:T(8,128)(2,1)S(1)} collective-permute-done((bf16[192,2048]{1,0:T(8,128)(2,1)S(1)}, bf16[192,2048]{1,0:T(8,128)(2,1)S(1)}, u32[]{:S(2)}, u32[]{:S(2)}) %collective-permute-start.29) | collective-permute-done | bytes 786464 | tf_op jit(solution)/shard_map/ppermute | solution.py:107
  314.0 16.8 %fusion.176 = f32[1536,2048]{1,0:T(8,128)} fusion(bf16[1536,2048]{1,0:T(8,128)(2,1)S(1)} %copy-done.68, bf16[384,1536]{1,0:T(8,128)(2,1)S(1)} %collective-permute-done.22, bf16[384,1536]{1,0:T(8,128)(2,1)S(1)} %collective-permute-done.21, bf16[384,1536]{1,0:T(8,128)(2,1)S(1)} %collective-permute-done.20, bf16[384,1536]{1,0:T(8,128)(2,1)S(1)} %fusion.47), kind=kOutput, calls=%fused_computation.319 | convolution fusion | flops 9682550784 | bytes 23592960 | tf_op jit(solution)/shard_map/dot_general | solution.py:55
  330.8 15.0 %multiply_convert_fusion.1 = (bf16[1536,1024]{1,0:T(8,128)(2,1)S(1)}, bf16[1536,1024]{1,0:T(8,128)(2,1)}, bf16[1536,1024]{1,0:T(8,128)(2,1)}) fusion(f32[1536,2048]{1,0:T(8,128)} %fusion.176, bf16[1536,1024]{1,0:T(8,128)(2,1)} %constant_dynamic-update-slice_fusion.31, bf16[384,1536]{1,0:T(8,128)(2,1)} %copy-done.42, bf16[384,1536]{1,0:T(8,128)(2,1)} %copy-done.41, ...), kind=kOutput, calls=%fused_computation.19 | convolution fusion | flops 4875878400 | bytes 29884416 | tf_op jit(solution)/shard_map/dot_general | solution.py:55
  345.8 6.8 fusion.92
  354.5 3.8 fusion.89
  359.8 15.1 %convolution_convert_fusion.1 = bf16[1536,1536]{1,0:T(8,128)(2,1)} fusion(bf16[1536,2048]{1,0:T(8,128)(2,1)} %constant_dynamic-update-slice_fusion.22, bf16[1536,1024]{1,0:T(8,128)(2,1)} %get-tuple-element.19, bf16[1536,1024]{1,0:T(8,128)(2,1)S(1)} %get-tuple-element.18), kind=kOutput, calls=%fused_computation.14 | convolution fusion | flops 9678618624 | bytes 17301504 | tf_op jit(solution)/shard_map/dot_general | solution.py:65
  374.9 3.8 fusion.86
  379.3 7.4 convolution_convert_fusion
  390.3 4.1 convert_add_fusion.3
  396.0 28.0 %collective-permute-done.59 = bf16[768,1024]{1,0:T(8,128)(2,1)} collective-permute-done((bf16[768,1024]{1,0:T(8,128)(2,1)}, bf16[768,1024]{1,0:T(8,128)(2,1)}, u32[]{:S(2)}, u32[]{:S(2)}) %collective-permute-start.59) | collective-permute-done | bytes 1572896 | tf_op jit(solution)/shard_map/ppermute | solution.py:107
  424.0 4.1 convert_add_fusion.4
  429.7 24.8 %collective-permute-done.56 = bf16[768,1024]{1,0:T(8,128)(2,1)S(1)} collective-permute-done((bf16[768,1024]{1,0:T(8,128)(2,1)}, bf16[768,1024]{1,0:T(8,128)(2,1)S(1)}, u32[]{:S(2)}, u32[]{:S(2)}) %collective-permute-start.56) | collective-permute-done | bytes 1572896 | tf_op jit(solution)/shard_map/ppermute | solution.py:107
  454.5 2.7 convert_add_fusion.5
  463.5 22.9 %collective-permute-done.57 = bf16[384,1024]{1,0:T(8,128)(2,1)S(1)} collective-permute-done((bf16[384,1024]{1,0:T(8,128)(2,1)S(1)}, bf16[384,1024]{1,0:T(8,128)(2,1)S(1)}, u32[]{:S(2)}, u32[]{:S(2)}) %collective-permute-start.57) | collective-permute-done | bytes 786464 | tf_op jit(solution)/shard_map/ppermute | solution.py:107
  496.8 9.9 %collective-permute-done.61 = bf16[192,1024]{1,0:T(8,128)(2,1)S(1)} collective-permute-done((bf16[192,1024]{1,0:T(8,128)(2,1)S(1)}, bf16[192,1024]{1,0:T(8,128)(2,1)S(1)}, u32[]{:S(2)}, u32[]{:S(2)}) %collective-permute-start.61) | collective-permute-done | bytes 393248 | tf_op jit(solution)/shard_map/ppermute | solution.py:107
  506.6 4.2 collective-permute-done.58
  512.9 29.6 %psum.7 = f32[192]{0:T(256)} all-reduce(f32[192]{0:T(256)} %get-tuple-element.11), channel_id=1, replica_groups=mesh['dp'=8,'tensor'=4] {'tensor'}, use_global_device_ids=true, to_apply=%region_12.13 | all-reduce | flops 192 | bytes 1536 | tf_op jit(solution)/shard_map/psum | solution.py:311
  546.0 4.5 multiply_reduce_fusion.1
  552.6 2.8 convolution_convert_fusion.5
  563.7 3.2 fusion.46
  566.9 6.2 reshape.247
  573.1 5.2 copy.140
  578.3 3.8 fusion.102
  599.7 3.3 fusion.178
  603.1 3.2 copy.167
  606.3 3.2 copy.168
  609.5 3.7 subtract_convert_fusion
  615.2 4.1 convert_element_type.310
  627.0 3.1 fusion.68
  630.0 3.1 fusion.66
  633.1 3.1 fusion.64
  636.2 3.1 fusion.62
  645.4 4.4 fusion.5
  649.9 69.7 %collective-permute-done.52 = bf16[384,1536]{1,0:T(8,128)(2,1)S(1)} collective-permute-done((bf16[384,1536]{1,0:T(8,128)(2,1)S(1)}, bf16[384,1536]{1,0:T(8,128)(2,1)S(1)}, u32[]{:S(2)}, u32[]{:S(2)}) %collective-permute-start.52) | collective-permute-done | bytes 1179680 | tf_op jit(solution)/shard_map/ppermute | solution.py:107
  724.5 6.1 fusion.40
  730.6 5.8 collective-permute-done.53
  736.5 2.7 collective-permute-start.54
  739.2 27.2 %collective-permute-done.47 = bf16[192,3072]{1,0:T(8,128)(2,1)S(1)} collective-permute-done((bf16[192,3072]{1,0:T(8,128)(2,1)S(1)}, bf16[192,3072]{1,0:T(8,128)(2,1)S(1)}, u32[]{:S(2)}, u32[]{:S(2)}) %collective-permute-start.47) | collective-permute-done | bytes 1179680 | tf_op jit(solution)/shard_map/ppermute | solution.py:107
  767.3 4.6 fusion.49
  773.4 20.7 %collective-permute-done.48 = bf16[96,3072]{1,0:T(8,128)(2,1)S(1)} collective-permute-done((bf16[96,3072]{1,0:T(8,128)(2,1)S(1)}, bf16[96,3072]{1,0:T(8,128)(2,1)S(1)}, u32[]{:S(2)}, u32[]{:S(2)}) %collective-permute-start.48) | collective-permute-done | bytes 589856 | tf_op jit(solution)/shard_map/ppermute | solution.py:107
  796.6 6.7 collective-permute-done.49
  (431 shorter events, 204.1 us)
Async XLA Ops:
  0.7 112.3 %collective-permute-start.30 = (bf16[192,1024]{1,0:T(8,128)(2,1)}, bf16[192,1024]{1,0:T(8,128)(2,1)}, u32[]{:S(2)}, u32[]{:S(2)}) collective-permute-start(bf16[192,1024]{1,0:T(8,128)(2,1)} %bitcast.152), channel_id=1, source_target_pairs={{0,16},{1,17},{2,18},{3,19},{4,20},{5,21},{6,22},{7,23},{8,24},{9,... | collective-permute-start | bytes 1179656 | tf_op jit(solution)/shard_map/ppermute | solution.py:107
  4.8 109.7 %collective-permute-start.31 = (bf16[192,1024]{1,0:T(8,128)(2,1)}, bf16[192,1024]{1,0:T(8,128)(2,1)}, u32[]{:S(2)}, u32[]{:S(2)}) collective-permute-start(bf16[192,1024]{1,0:T(8,128)(2,1)} %bitcast.153), channel_id=1, source_target_pairs={{0,8},{1,9},{2,10},{3,11},{4,12},{5,13},{6,14},{7,15},{8,0},{9,1},... | collective-permute-start | bytes 1179656 | tf_op jit(solution)/shard_map/ppermute | solution.py:107
  9.0 14.8 %collective-permute-start = (bf16[48,3200]{1,0:T(8,128)(2,1)S(1)}, bf16[48,3200]{1,0:T(8,128)(2,1)S(1)}, u32[]{:S(2)}, u32[]{:S(2)}) collective-permute-start(bf16[48,3200]{1,0:T(8,128)(2,1)S(1)} %get-tuple-element.40), channel_id=1, source_target_pairs={{0,4},{1,5},{2,6},{3,7},{4,0},{5,1},{6,2},{7,3},{8,12},{9,13},{10,... | collective-permute-start | bytes 921608 | tf_op jit(solution)/shard_map/ppermute | solution.py:107
  10.5 14.9 %collective-permute-start.10 = (bf16[48,1536]{1,0:T(8,128)(2,1)}, bf16[48,1536]{1,0:T(8,128)(2,1)S(1)}, u32[]{:S(2)}, u32[]{:S(2)}) collective-permute-start(bf16[48,1536]{1,0:T(8,128)(2,1)} %param.18), channel_id=1, source_target_pairs={{0,4},{1,5},{2,6},{3,7},{4,0},{5,1},{6,2},{7,3},{8,12},{9,13},{10,... | collective-permute-start | bytes 442376 | tf_op jit(solution)/shard_map/ppermute | solution.py:107
  23.9 14.5 %collective-permute-start.4 = (bf16[96,3200]{1,0:T(8,128)(2,1)S(1)}, bf16[96,3200]{1,0:T(8,128)(2,1)S(1)}, u32[]{:S(2)}, u32[]{:S(2)}) collective-permute-start(bf16[96,3200]{1,0:T(8,128)(2,1)S(1)} %pad_maximum_fusion.6), channel_id=1, source_target_pairs={{0,2},{1,3},{2,0},{3,1},{4,6},{5,7},{6,4},{7,5},{8,10},{9,11},{10,... | collective-permute-start | bytes 1843208 | tf_op jit(solution)/shard_map/ppermute | solution.py:107
  26.1 90.0 %collective-permute-start.11 = (bf16[96,1536]{1,0:T(8,128)(2,1)}, bf16[96,1536]{1,0:T(8,128)(2,1)S(1)}, u32[]{:S(2)}, u32[]{:S(2)}) collective-permute-start(bf16[96,1536]{1,0:T(8,128)(2,1)} %get-tuple-element.42), channel_id=1, source_target_pairs={{0,16},{1,17},{2,18},{3,19},{4,20},{5,21},{6,22},{7,23},{8,24},{9,... | collective-permute-start | bytes 884744 | tf_op jit(solution)/shard_map/ppermute | solution.py:107
  26.5 40.8 %collective-permute-start.1 = (bf16[96,3200]{1,0:T(8,128)(2,1)S(1)}, bf16[96,3200]{1,0:T(8,128)(2,1)S(1)}, u32[]{:S(2)}, u32[]{:S(2)}) collective-permute-start(bf16[96,3200]{1,0:T(8,128)(2,1)S(1)} %pad_maximum_fusion.6), channel_id=1, source_target_pairs={{0,16},{1,17},{2,18},{3,19},{4,20},{5,21},{6,22},{7,23},{8,24},{9,... | collective-permute-start | bytes 1843208 | tf_op jit(solution)/shard_map/ppermute | solution.py:107
  38.4 34.4 %collective-permute-start.2 = (bf16[96,3200]{1,0:T(8,128)(2,1)S(1)}, bf16[96,3200]{1,0:T(8,128)(2,1)S(1)}, u32[]{:S(2)}, u32[]{:S(2)}) collective-permute-start(bf16[96,3200]{1,0:T(8,128)(2,1)S(1)} %pad_maximum_fusion.6), channel_id=1, source_target_pairs={{0,8},{1,9},{2,10},{3,11},{4,12},{5,13},{6,14},{7,15},{8,0},{9,1},... | collective-permute-start | bytes 1843208 | tf_op jit(solution)/shard_map/ppermute | solution.py:107
  67.2 17.3 %collective-permute-start.3 = (bf16[96,3200]{1,0:T(8,128)(2,1)S(1)}, bf16[96,3200]{1,0:T(8,128)(2,1)S(1)}, u32[]{:S(2)}, u32[]{:S(2)}) collective-permute-start(bf16[96,3200]{1,0:T(8,128)(2,1)S(1)} %collective-permute-done.1), channel_id=1, source_target_pairs={{0,8},{1,9},{2,10},{3,11},{4,12},{5,13},{6,14},{7,15},{8,0},{9,1},... | collective-permute-start | bytes 1843208 | tf_op jit(solution)/shard_map/ppermute | solution.py:107
  72.8 14.1 %collective-permute-start.5 = (bf16[96,3200]{1,0:T(8,128)(2,1)S(1)}, bf16[96,3200]{1,0:T(8,128)(2,1)S(1)}, u32[]{:S(2)}, u32[]{:S(2)}) collective-permute-start(bf16[96,3200]{1,0:T(8,128)(2,1)S(1)} %collective-permute-done.1), channel_id=1, source_target_pairs={{0,2},{1,3},{2,0},{3,1},{4,6},{5,7},{6,4},{7,5},{8,10},{9,11},{10,... | collective-permute-start | bytes 1843208 | tf_op jit(solution)/shard_map/ppermute | solution.py:107
  84.5 16.8 %collective-permute-start.6 = (bf16[96,3200]{1,0:T(8,128)(2,1)S(1)}, bf16[96,3200]{1,0:T(8,128)(2,1)S(1)}, u32[]{:S(2)}, u32[]{:S(2)}) collective-permute-start(bf16[96,3200]{1,0:T(8,128)(2,1)S(1)} %collective-permute-done.2), channel_id=1, source_target_pairs={{0,2},{1,3},{2,0},{3,1},{4,6},{5,7},{6,4},{7,5},{8,10},{9,11},{10,... | collective-permute-start | bytes 1843208 | tf_op jit(solution)/shard_map/ppermute | solution.py:107
  86.9 25.2 %collective-permute-start.7 = (bf16[96,3200]{1,0:T(8,128)(2,1)S(1)}, bf16[96,3200]{1,0:T(8,128)(2,1)S(1)}, u32[]{:S(2)}, u32[]{:S(2)}) collective-permute-start(bf16[96,3200]{1,0:T(8,128)(2,1)S(1)} %collective-permute-done.3), channel_id=1, source_target_pairs={{0,2},{1,3},{2,0},{3,1},{4,6},{5,7},{6,4},{7,5},{8,10},{9,11},{10,... | collective-permute-start | bytes 1843208 | tf_op jit(solution)/shard_map/ppermute | solution.py:107
  101.3 15.7 %collective-permute-start.12 = (bf16[96,1536]{1,0:T(8,128)(2,1)}, bf16[96,1536]{1,0:T(8,128)(2,1)S(1)}, u32[]{:S(2)}, u32[]{:S(2)}) collective-permute-start(bf16[96,1536]{1,0:T(8,128)(2,1)} %get-tuple-element.42), channel_id=1, source_target_pairs={{0,8},{1,9},{2,10},{3,11},{4,12},{5,13},{6,14},{7,15},{8,0},{9,1},... | collective-permute-start | bytes 884744 | tf_op jit(solution)/shard_map/ppermute | solution.py:107
  112.1 65.9 %collective-permute-start.8 = (bf16[384,3200]{1,0:T(8,128)(2,1)}, bf16[384,3200]{1,0:T(8,128)(2,1)}, u32[]{:S(2)}, u32[]{:S(2)}) collective-permute-start(bf16[384,3200]{1,0:T(8,128)(2,1)} %constant_dynamic-update-slice_fusion), channel_id=1, source_target_pairs={{0,1},{1,0},{2,3},{3,2},{4,5},{5,4},{6,7},{7,6},{8,9},{9,8},{10,11... | collective-permute-start | bytes 7372808 | tf_op jit(solution)/shard_map/ppermute | solution.py:107
  112.9 66.1 %collective-permute-start.9 = (bf16[384,3200]{1,0:T(8,128)(2,1)}, bf16[384,3200]{1,0:T(8,128)(2,1)}, u32[]{:S(2)}, u32[]{:S(2)}) collective-permute-start(bf16[384,3200]{1,0:T(8,128)(2,1)} %constant_dynamic-update-slice_fusion.5), channel_id=1, source_target_pairs={{0,1},{1,0},{2,3},{3,2},{4,5},{5,4},{6,7},{7,6},{8,9},{9,8},{10,11... | collective-permute-start | bytes 7372808 | tf_op jit(solution)/shard_map/ppermute | solution.py:107
  114.5 10.2 %collective-permute-start.14 = (bf16[96,1536]{1,0:T(8,128)(2,1)}, bf16[96,1536]{1,0:T(8,128)(2,1)S(1)}, u32[]{:S(2)}, u32[]{:S(2)}) collective-permute-start(bf16[96,1536]{1,0:T(8,128)(2,1)} %get-tuple-element.42), channel_id=1, source_target_pairs={{0,2},{1,3},{2,0},{3,1},{4,6},{5,7},{6,4},{7,5},{8,10},{9,11},{10,... | collective-permute-start | bytes 884744 | tf_op jit(solution)/shard_map/ppermute | solution.py:107
  116.1 9.8 %collective-permute-start.13 = (bf16[96,1536]{1,0:T(8,128)(2,1)S(1)}, bf16[96,1536]{1,0:T(8,128)(2,1)S(1)}, u32[]{:S(2)}, u32[]{:S(2)}) collective-permute-start(bf16[96,1536]{1,0:T(8,128)(2,1)S(1)} %collective-permute-done.11), channel_id=1, source_target_pairs={{0,8},{1,9},{2,10},{3,11},{4,12},{5,13},{6,14},{7,15},{8,0},{9,1},... | collective-permute-start | bytes 884744 | tf_op jit(solution)/shard_map/ppermute | solution.py:107
  117.0 14.0 %collective-permute-start.15 = (bf16[96,1536]{1,0:T(8,128)(2,1)S(1)}, bf16[96,1536]{1,0:T(8,128)(2,1)S(1)}, u32[]{:S(2)}, u32[]{:S(2)}) collective-permute-start(bf16[96,1536]{1,0:T(8,128)(2,1)S(1)} %collective-permute-done.11), channel_id=1, source_target_pairs={{0,2},{1,3},{2,0},{3,1},{4,6},{5,7},{6,4},{7,5},{8,10},{9,11},{10,... | collective-permute-start | bytes 884744 | tf_op jit(solution)/shard_map/ppermute | solution.py:107
  124.6 11.7 %collective-permute-start.16 = (bf16[96,1536]{1,0:T(8,128)(2,1)S(1)}, bf16[96,1536]{1,0:T(8,128)(2,1)S(1)}, u32[]{:S(2)}, u32[]{:S(2)}) collective-permute-start(bf16[96,1536]{1,0:T(8,128)(2,1)S(1)} %collective-permute-done.12), channel_id=1, source_target_pairs={{0,2},{1,3},{2,0},{3,1},{4,6},{5,7},{6,4},{7,5},{8,10},{9,11},{10,... | collective-permute-start | bytes 884744 | tf_op jit(solution)/shard_map/ppermute | solution.py:107
  126.0 11.1 %collective-permute-start.32 = (bf16[192,1024]{1,0:T(8,128)(2,1)}, bf16[192,1024]{1,0:T(8,128)(2,1)S(1)}, u32[]{:S(2)}, u32[]{:S(2)}) collective-permute-start(bf16[192,1024]{1,0:T(8,128)(2,1)} %collective-permute-done.30), channel_id=1, source_target_pairs={{0,8},{1,9},{2,10},{3,11},{4,12},{5,13},{6,14},{7,15},{8,0},{9,1},... | collective-permute-start | bytes 1179656 | tf_op jit(solution)/shard_map/ppermute | solution.py:107
  131.0 10.3 %collective-permute-start.33 = (bf16[192,1024]{1,0:T(8,128)(2,1)S(1)}, bf16[192,1024]{1,0:T(8,128)(2,1)S(1)}, u32[]{:S(2)}, u32[]{:S(2)}) collective-permute-start(bf16[192,1024]{1,0:T(8,128)(2,1)S(1)} %bitcast.154), channel_id=1, source_target_pairs={{0,4},{1,5},{2,6},{3,7},{4,0},{5,1},{6,2},{7,3},{8,12},{9,13},{10,... | collective-permute-start | bytes 1179656 | tf_op jit(solution)/shard_map/ppermute | solution.py:107
  136.3 35.9 %collective-permute-start.23 = (bf16[192,2048]{1,0:T(8,128)(2,1)}, bf16[192,2048]{1,0:T(8,128)(2,1)S(1)}, u32[]{:S(2)}, u32[]{:S(2)}) collective-permute-start(bf16[192,2048]{1,0:T(8,128)(2,1)} %get-tuple-element.35), channel_id=1, source_target_pairs={{0,16},{1,17},{2,18},{3,19},{4,20},{5,21},{6,22},{7,23},{8,24},{9,... | collective-permute-start | bytes 2359304 | tf_op jit(solution)/shard_map/ppermute | solution.py:107
  137.1 11.5 %collective-permute-start.34 = (bf16[192,1024]{1,0:T(8,128)(2,1)}, bf16[192,1024]{1,0:T(8,128)(2,1)S(1)}, u32[]{:S(2)}, u32[]{:S(2)}) collective-permute-start(bf16[192,1024]{1,0:T(8,128)(2,1)} %collective-permute-done.30), channel_id=1, source_target_pairs={{0,4},{1,5},{2,6},{3,7},{4,0},{5,1},{6,2},{7,3},{8,12},{9,13},{10,... | collective-permute-start | bytes 1179656 | tf_op jit(solution)/shard_map/ppermute | solution.py:107
  141.3 104.0 %collective-permute-start.24 = (bf16[192,2048]{1,0:T(8,128)(2,1)}, bf16[192,2048]{1,0:T(8,128)(2,1)}, u32[]{:S(2)}, u32[]{:S(2)}) collective-permute-start(bf16[192,2048]{1,0:T(8,128)(2,1)} %get-tuple-element.35), channel_id=1, source_target_pairs={{0,8},{1,9},{2,10},{3,11},{4,12},{5,13},{6,14},{7,15},{8,0},{9,1},... | collective-permute-start | bytes 2359304 | tf_op jit(solution)/shard_map/ppermute | solution.py:107
  148.6 26.1 %collective-permute-start.17 = (bf16[96,1536]{1,0:T(8,128)(2,1)S(1)}, bf16[96,1536]{1,0:T(8,128)(2,1)S(1)}, u32[]{:S(2)}, u32[]{:S(2)}) collective-permute-start(bf16[96,1536]{1,0:T(8,128)(2,1)S(1)} %collective-permute-done.13), channel_id=1, source_target_pairs={{0,2},{1,3},{2,0},{3,1},{4,6},{5,7},{6,4},{7,5},{8,10},{9,11},{10,... | collective-permute-start | bytes 884744 | tf_op jit(solution)/shard_map/ppermute | solution.py:107
  172.3 74.5 %collective-permute-start.26 = (bf16[192,2048]{1,0:T(8,128)(2,1)}, bf16[192,2048]{1,0:T(8,128)(2,1)}, u32[]{:S(2)}, u32[]{:S(2)}) collective-permute-start(bf16[192,2048]{1,0:T(8,128)(2,1)} %get-tuple-element.35), channel_id=1, source_target_pairs={{0,4},{1,5},{2,6},{3,7},{4,0},{5,1},{6,2},{7,3},{8,12},{9,13},{10,... | collective-permute-start | bytes 2359304 | tf_op jit(solution)/shard_map/ppermute | solution.py:107
  174.7 100.4 %collective-permute-start.39 = (bf16[384,1536]{1,0:T(8,128)(2,1)}, bf16[384,1536]{1,0:T(8,128)(2,1)}, u32[]{:S(2)}, u32[]{:S(2)}) collective-permute-start(bf16[384,1536]{1,0:T(8,128)(2,1)} %fusion.57), channel_id=1, source_target_pairs={{0,2},{1,3},{2,0},{3,1},{4,6},{5,7},{6,4},{7,5},{8,10},{9,11},{10,... | collective-permute-start | bytes 3538952 | tf_op jit(solution)/shard_map/ppermute | solution.py:107
  178.0 58.2 %collective-permute-start.18 = (bf16[384,1536]{1,0:T(8,128)(2,1)}, bf16[384,1536]{1,0:T(8,128)(2,1)}, u32[]{:S(2)}, u32[]{:S(2)}) collective-permute-start(bf16[384,1536]{1,0:T(8,128)(2,1)} %constant_dynamic-update-slice_fusion.11), channel_id=1, source_target_pairs={{0,1},{1,0},{2,3},{3,2},{4,5},{5,4},{6,7},{7,6},{8,9},{9,8},{10,11... | collective-permute-start | bytes 3538952 | tf_op jit(solution)/shard_map/ppermute | solution.py:107
  179.1 59.8 %collective-permute-start.19 = (bf16[384,1536]{1,0:T(8,128)(2,1)}, bf16[384,1536]{1,0:T(8,128)(2,1)}, u32[]{:S(2)}, u32[]{:S(2)}) collective-permute-start(bf16[384,1536]{1,0:T(8,128)(2,1)} %constant_dynamic-update-slice_fusion.16), channel_id=1, source_target_pairs={{0,1},{1,0},{2,3},{3,2},{4,5},{5,4},{6,7},{7,6},{8,9},{9,8},{10,11... | collective-permute-start | bytes 3538952 | tf_op jit(solution)/shard_map/ppermute | solution.py:107
  236.2 13.4 %collective-permute-start.35 = (bf16[192,1024]{1,0:T(8,128)(2,1)}, bf16[192,1024]{1,0:T(8,128)(2,1)S(1)}, u32[]{:S(2)}, u32[]{:S(2)}) collective-permute-start(bf16[192,1024]{1,0:T(8,128)(2,1)} %collective-permute-done.31), channel_id=1, source_target_pairs={{0,4},{1,5},{2,6},{3,7},{4,0},{5,1},{6,2},{7,3},{8,12},{9,13},{10,... | collective-permute-start | bytes 1179656 | tf_op jit(solution)/shard_map/ppermute | solution.py:107
  238.9 36.3 %collective-permute-start.25 = (bf16[192,2048]{1,0:T(8,128)(2,1)S(1)}, bf16[192,2048]{1,0:T(8,128)(2,1)S(1)}, u32[]{:S(2)}, u32[]{:S(2)}) collective-permute-start(bf16[192,2048]{1,0:T(8,128)(2,1)S(1)} %copy-done.51), channel_id=1, source_target_pairs={{0,8},{1,9},{2,10},{3,11},{4,12},{5,13},{6,14},{7,15},{8,0},{9,1},... | collective-permute-start | bytes 2359304 | tf_op jit(solution)/shard_map/ppermute | solution.py:107
  245.2 30.5 %collective-permute-start.27 = (bf16[192,2048]{1,0:T(8,128)(2,1)S(1)}, bf16[192,2048]{1,0:T(8,128)(2,1)S(1)}, u32[]{:S(2)}, u32[]{:S(2)}) collective-permute-start(bf16[192,2048]{1,0:T(8,128)(2,1)S(1)} %copy-done.51), channel_id=1, source_target_pairs={{0,4},{1,5},{2,6},{3,7},{4,0},{5,1},{6,2},{7,3},{8,12},{9,13},{10,... | collective-permute-start | bytes 2359304 | tf_op jit(solution)/shard_map/ppermute | solution.py:107
  246.8 26.1 %collective-permute-start.36 = (bf16[192,1024]{1,0:T(8,128)(2,1)S(1)}, bf16[192,1024]{1,0:T(8,128)(2,1)S(1)}, u32[]{:S(2)}, u32[]{:S(2)}) collective-permute-start(bf16[192,1024]{1,0:T(8,128)(2,1)S(1)} %copy-done.62), channel_id=1, source_target_pairs={{0,4},{1,5},{2,6},{3,7},{4,0},{5,1},{6,2},{7,3},{8,12},{9,13},{10,... | collective-permute-start | bytes 1179656 | tf_op jit(solution)/shard_map/ppermute | solution.py:107
  249.6 44.0 %collective-permute-start.20 = (bf16[384,1536]{1,0:T(8,128)(2,1)S(1)}, bf16[384,1536]{1,0:T(8,128)(2,1)S(1)}, u32[]{:S(2)}, u32[]{:S(2)}) collective-permute-start(bf16[384,1536]{1,0:T(8,128)(2,1)S(1)} %fusion.47), channel_id=1, source_target_pairs={{0,2},{1,3},{2,0},{3,1},{4,6},{5,7},{6,4},{7,5},{8,10},{9,11},{10,... | collective-permute-start | bytes 3538952 | tf_op jit(solution)/shard_map/ppermute | solution.py:107
  272.9 20.7 %collective-permute-start.28 = (bf16[192,2048]{1,0:T(8,128)(2,1)}, bf16[192,2048]{1,0:T(8,128)(2,1)S(1)}, u32[]{:S(2)}, u32[]{:S(2)}) collective-permute-start(bf16[192,2048]{1,0:T(8,128)(2,1)} %collective-permute-done.24), channel_id=1, source_target_pairs={{0,4},{1,5},{2,6},{3,7},{4,0},{5,1},{6,2},{7,3},{8,12},{9,13},{10,... | collective-permute-start | bytes 2359304 | tf_op jit(solution)/shard_map/ppermute | solution.py:107
  275.2 34.0 %collective-permute-start.40 = (bf16[384,1536]{1,0:T(8,128)(2,1)}, bf16[384,1536]{1,0:T(8,128)(2,1)S(1)}, u32[]{:S(2)}, u32[]{:S(2)}) collective-permute-start(bf16[384,1536]{1,0:T(8,128)(2,1)} %fusion.57), channel_id=1, source_target_pairs={{0,1},{1,0},{2,3},{3,2},{4,5},{5,4},{6,7},{7,6},{8,9},{9,8},{10,11... | collective-permute-start | bytes 3538952 | tf_op jit(solution)/shard_map/ppermute | solution.py:107
  275.2 34.0 %collective-permute-start.41 = (bf16[384,1536]{1,0:T(8,128)(2,1)}, bf16[384,1536]{1,0:T(8,128)(2,1)S(1)}, u32[]{:S(2)}, u32[]{:S(2)}) collective-permute-start(bf16[384,1536]{1,0:T(8,128)(2,1)} %collective-permute-done.39), channel_id=1, source_target_pairs={{0,1},{1,0},{2,3},{3,2},{4,5},{5,4},{6,7},{7,6},{8,9},{9,8},{10,11... | collective-permute-start | bytes 3538952 | tf_op jit(solution)/shard_map/ppermute | solution.py:107
  275.7 32.6 %collective-permute-start.29 = (bf16[192,2048]{1,0:T(8,128)(2,1)S(1)}, bf16[192,2048]{1,0:T(8,128)(2,1)S(1)}, u32[]{:S(2)}, u32[]{:S(2)}) collective-permute-start(bf16[192,2048]{1,0:T(8,128)(2,1)S(1)} %collective-permute-done.25), channel_id=1, source_target_pairs={{0,4},{1,5},{2,6},{3,7},{4,0},{5,1},{6,2},{7,3},{8,12},{9,13},{10,... | collective-permute-start | bytes 2359304 | tf_op jit(solution)/shard_map/ppermute | solution.py:107
  293.6 18.3 %collective-permute-start.21 = (bf16[384,1536]{1,0:T(8,128)(2,1)S(1)}, bf16[384,1536]{1,0:T(8,128)(2,1)S(1)}, u32[]{:S(2)}, u32[]{:S(2)}) collective-permute-start(bf16[384,1536]{1,0:T(8,128)(2,1)S(1)} %fusion.47), channel_id=1, source_target_pairs={{0,1},{1,0},{2,3},{3,2},{4,5},{5,4},{6,7},{7,6},{8,9},{9,8},{10,11... | collective-permute-start | bytes 3538952 | tf_op jit(solution)/shard_map/ppermute | solution.py:107
  293.6 18.4 %collective-permute-start.22 = (bf16[384,1536]{1,0:T(8,128)(2,1)S(1)}, bf16[384,1536]{1,0:T(8,128)(2,1)S(1)}, u32[]{:S(2)}, u32[]{:S(2)}) collective-permute-start(bf16[384,1536]{1,0:T(8,128)(2,1)S(1)} %collective-permute-done.20), channel_id=1, source_target_pairs={{0,1},{1,0},{2,3},{3,2},{4,5},{5,4},{6,7},{7,6},{8,9},{9,8},{10,11... | collective-permute-start | bytes 3538952 | tf_op jit(solution)/shard_map/ppermute | solution.py:107
  352.7 37.6 %collective-permute-start.62 = (bf16[768,1024]{1,0:T(8,128)(2,1)}, bf16[768,1024]{1,0:T(8,128)(2,1)}, u32[]{:S(2)}, u32[]{:S(2)}) collective-permute-start(bf16[768,1024]{1,0:T(8,128)(2,1)} %fusion.92), channel_id=1, source_target_pairs={{0,4},{1,5},{2,6},{3,7},{4,0},{5,1},{6,2},{7,3},{8,12},{9,13},{10,... | collective-permute-start | bytes 4718600 | tf_op jit(solution)/shard_map/ppermute | solution.py:107
  358.3 65.7 %collective-permute-start.59 = (bf16[768,1024]{1,0:T(8,128)(2,1)}, bf16[768,1024]{1,0:T(8,128)(2,1)}, u32[]{:S(2)}, u32[]{:S(2)}) collective-permute-start(bf16[768,1024]{1,0:T(8,128)(2,1)} %fusion.89), channel_id=1, source_target_pairs={{0,4},{1,5},{2,6},{3,7},{4,0},{5,1},{6,2},{7,3},{8,12},{9,13},{10,... | collective-permute-start | bytes 4718600 | tf_op jit(solution)/shard_map/ppermute | solution.py:107
  378.7 75.8 %collective-permute-start.56 = (bf16[768,1024]{1,0:T(8,128)(2,1)}, bf16[768,1024]{1,0:T(8,128)(2,1)S(1)}, u32[]{:S(2)}, u32[]{:S(2)}) collective-permute-start(bf16[768,1024]{1,0:T(8,128)(2,1)} %fusion.86), channel_id=1, source_target_pairs={{0,4},{1,5},{2,6},{3,7},{4,0},{5,1},{6,2},{7,3},{8,12},{9,13},{10,... | collective-permute-start | bytes 4718600 | tf_op jit(solution)/shard_map/ppermute | solution.py:107
  386.8 100.3 %collective-permute-start.42 = (bf16[768,1536]{1,0:T(8,128)(2,1)S(1)}, bf16[768,1536]{1,0:T(8,128)(2,1)}, u32[]{:S(2)}, u32[]{:S(2)}) collective-permute-start(bf16[768,1536]{1,0:T(8,128)(2,1)S(1)} %slice.327), channel_id=1, source_target_pairs={{0,1},{1,0},{2,3},{3,2},{4,5},{5,4},{6,7},{7,6},{8,9},{9,8},{10,11... | collective-permute-start | bytes 7077896 | tf_op jit(solution)/shard_map/ppermute | solution.py:107
  387.1 104.6 %collective-permute-start.37 = (bf16[768,1536]{1,0:T(8,128)(2,1)S(1)}, bf16[768,1536]{1,0:T(8,128)(2,1)}, u32[]{:S(2)}, u32[]{:S(2)}) collective-permute-start(bf16[768,1536]{1,0:T(8,128)(2,1)S(1)} %slice.323), channel_id=1, source_target_pairs={{0,1},{1,0},{2,3},{3,2},{4,5},{5,4},{6,7},{7,6},{8,9},{9,8},{10,11... | collective-permute-start | bytes 7077896 | tf_op jit(solution)/shard_map/ppermute | solution.py:107
  394.6 64.4 %collective-permute-start.63 = (bf16[384,1024]{1,0:T(8,128)(2,1)S(1)}, bf16[384,1024]{1,0:T(8,128)(2,1)S(1)}, u32[]{:S(2)}, u32[]{:S(2)}) collective-permute-start(bf16[384,1024]{1,0:T(8,128)(2,1)S(1)} %slice.497), channel_id=1, source_target_pairs={{0,8},{1,9},{2,10},{3,11},{4,12},{5,13},{6,14},{7,15},{8,0},{9,1},... | collective-permute-start | bytes 2359304 | tf_op jit(solution)/shard_map/ppermute | solution.py:107
  428.3 32.3 %collective-permute-start.60 = (bf16[384,1024]{1,0:T(8,128)(2,1)S(1)}, bf16[384,1024]{1,0:T(8,128)(2,1)S(1)}, u32[]{:S(2)}, u32[]{:S(2)}) collective-permute-start(bf16[384,1024]{1,0:T(8,128)(2,1)S(1)} %slice.498), channel_id=1, source_target_pairs={{0,8},{1,9},{2,10},{3,11},{4,12},{5,13},{6,14},{7,15},{8,0},{9,1},... | collective-permute-start | bytes 2359304 | tf_op jit(solution)/shard_map/ppermute | solution.py:107
  457.4 29.1 %collective-permute-start.57 = (bf16[384,1024]{1,0:T(8,128)(2,1)S(1)}, bf16[384,1024]{1,0:T(8,128)(2,1)S(1)}, u32[]{:S(2)}, u32[]{:S(2)}) collective-permute-start(bf16[384,1024]{1,0:T(8,128)(2,1)S(1)} %slice.499), channel_id=1, source_target_pairs={{0,8},{1,9},{2,10},{3,11},{4,12},{5,13},{6,14},{7,15},{8,0},{9,1},... | collective-permute-start | bytes 2359304 | tf_op jit(solution)/shard_map/ppermute | solution.py:107
  460.2 83.6 %collective-permute-start.64 = (bf16[192,1024]{1,0:T(8,128)(2,1)}, bf16[192,1024]{1,0:T(8,128)(2,1)}, u32[]{:S(2)}, u32[]{:S(2)}) collective-permute-start(bf16[192,1024]{1,0:T(8,128)(2,1)} %slice.503), channel_id=1, source_target_pairs={{0,16},{1,17},{2,18},{3,19},{4,20},{5,21},{6,22},{7,23},{8,24},{9,... | collective-permute-start | bytes 1179656 | tf_op jit(solution)/shard_map/ppermute | solution.py:107
  460.9 45.7 %collective-permute-start.61 = (bf16[192,1024]{1,0:T(8,128)(2,1)S(1)}, bf16[192,1024]{1,0:T(8,128)(2,1)S(1)}, u32[]{:S(2)}, u32[]{:S(2)}) collective-permute-start(bf16[192,1024]{1,0:T(8,128)(2,1)S(1)} %slice.504), channel_id=1, source_target_pairs={{0,16},{1,17},{2,18},{3,19},{4,20},{5,21},{6,22},{7,23},{8,24},{9,... | collective-permute-start | bytes 1179656 | tf_op jit(solution)/shard_map/ppermute | solution.py:107
  486.7 24.1 %collective-permute-start.58 = (bf16[192,1024]{1,0:T(8,128)(2,1)S(1)}, bf16[192,1024]{1,0:T(8,128)(2,1)S(1)}, u32[]{:S(2)}, u32[]{:S(2)}) collective-permute-start(bf16[192,1024]{1,0:T(8,128)(2,1)S(1)} %slice.505), channel_id=1, source_target_pairs={{0,16},{1,17},{2,18},{3,19},{4,20},{5,21},{6,22},{7,23},{8,24},{9,... | collective-permute-start | bytes 1179656 | tf_op jit(solution)/shard_map/ppermute | solution.py:107
  489.6 56.4 %collective-permute-start.43 = (bf16[384,1536]{1,0:T(8,128)(2,1)S(1)}, bf16[384,1536]{1,0:T(8,128)(2,1)}, u32[]{:S(2)}, u32[]{:S(2)}) collective-permute-start(bf16[384,1536]{1,0:T(8,128)(2,1)S(1)} %slice.495), channel_id=1, source_target_pairs={{0,2},{1,3},{2,0},{3,1},{4,6},{5,7},{6,4},{7,5},{8,10},{9,11},{10,... | collective-permute-start | bytes 3538952 | tf_op jit(solution)/shard_map/ppermute | solution.py:107
  495.3 272.0 %collective-permute-start.38 = (bf16[384,1536]{1,0:T(8,128)(2,1)}, bf16[384,1536]{1,0:T(8,128)(2,1)}, u32[]{:S(2)}, u32[]{:S(2)}) collective-permute-start(bf16[384,1536]{1,0:T(8,128)(2,1)} %slice.496), channel_id=1, source_target_pairs={{0,2},{1,3},{2,0},{3,1},{4,6},{5,7},{6,4},{7,5},{8,10},{9,11},{10,... | collective-permute-start | bytes 3538952 | tf_op jit(solution)/shard_map/ppermute | solution.py:107
  622.7 16.6 %collective-permute-start.45 = (bf16[384,3072]{1,0:T(8,128)(2,1)S(1)}, bf16[384,3072]{1,0:T(8,128)(2,1)S(1)}, u32[]{:S(2)}, u32[]{:S(2)}) collective-permute-start(bf16[384,3072]{1,0:T(8,128)(2,1)S(1)} %convolution_convert_fusion.2), channel_id=1, source_target_pairs={{0,1},{1,0},{2,3},{3,2},{4,5},{5,4},{6,7},{7,6},{8,9},{9,8},{10,11... | collective-permute-start | bytes 7077896 | tf_op jit(solution)/shard_map/ppermute | solution.py:107
  624.0 25.9 %collective-permute-start.50 = (bf16[384,1536]{1,0:T(8,128)(2,1)S(1)}, bf16[384,1536]{1,0:T(8,128)(2,1)S(1)}, u32[]{:S(2)}, u32[]{:S(2)}) collective-permute-start(bf16[384,1536]{1,0:T(8,128)(2,1)S(1)} %copy-done.47), channel_id=1, source_target_pairs={{0,1},{1,0},{2,3},{3,2},{4,5},{5,4},{6,7},{7,6},{8,9},{9,8},{10,11... | collective-permute-start | bytes 3538952 | tf_op jit(solution)/shard_map/ppermute | solution.py:107
  624.2 17.5 %collective-permute-start.51 = (bf16[384,1536]{1,0:T(8,128)(2,1)S(1)}, bf16[384,1536]{1,0:T(8,128)(2,1)S(1)}, u32[]{:S(2)}, u32[]{:S(2)}) collective-permute-start(bf16[384,1536]{1,0:T(8,128)(2,1)S(1)} %convolution_convert_fusion.4), channel_id=1, source_target_pairs={{0,1},{1,0},{2,3},{3,2},{4,5},{5,4},{6,7},{7,6},{8,9},{9,8},{10,11... | collective-permute-start | bytes 3538952 | tf_op jit(solution)/shard_map/ppermute | solution.py:107
  625.9 95.8 %collective-permute-start.44 = (bf16[384,3072]{1,0:T(8,128)(2,1)S(1)}, bf16[384,3072]{1,0:T(8,128)(2,1)S(1)}, u32[]{:S(2)}, u32[]{:S(2)}) collective-permute-start(bf16[384,3072]{1,0:T(8,128)(2,1)S(1)} %convolution_convert_fusion.3), channel_id=1, source_target_pairs={{0,1},{1,0},{2,3},{3,2},{4,5},{5,4},{6,7},{7,6},{8,9},{9,8},{10,11... | collective-permute-start | bytes 7077896 | tf_op jit(solution)/shard_map/ppermute | solution.py:107
  640.7 80.9 %collective-permute-start.46 = (bf16[384,3072]{1,0:T(8,128)(2,1)S(1)}, bf16[384,3072]{1,0:T(8,128)(2,1)S(1)}, u32[]{:S(2)}, u32[]{:S(2)}) collective-permute-start(bf16[384,3072]{1,0:T(8,128)(2,1)S(1)} %add_convert_fusion), channel_id=1, source_target_pairs={{0,2},{1,3},{2,0},{3,1},{4,6},{5,7},{6,4},{7,5},{8,10},{9,11},{10,... | collective-permute-start | bytes 7077896 | tf_op jit(solution)/shard_map/ppermute | solution.py:107
  642.5 77.0 %collective-permute-start.52 = (bf16[384,1536]{1,0:T(8,128)(2,1)S(1)}, bf16[384,1536]{1,0:T(8,128)(2,1)S(1)}, u32[]{:S(2)}, u32[]{:S(2)}) collective-permute-start(bf16[384,1536]{1,0:T(8,128)(2,1)S(1)} %add_convert_fusion.3), channel_id=1, source_target_pairs={{0,2},{1,3},{2,0},{3,1},{4,6},{5,7},{6,4},{7,5},{8,10},{9,11},{10,... | collective-permute-start | bytes 3538952 | tf_op jit(solution)/shard_map/ppermute | solution.py:107
  720.0 16.3 %collective-permute-start.53 = (bf16[192,1536]{1,0:T(8,128)(2,1)S(1)}, bf16[192,1536]{1,0:T(8,128)(2,1)S(1)}, u32[]{:S(2)}, u32[]{:S(2)}) collective-permute-start(bf16[192,1536]{1,0:T(8,128)(2,1)S(1)} %slice.500), channel_id=1, source_target_pairs={{0,8},{1,9},{2,10},{3,11},{4,12},{5,13},{6,14},{7,15},{8,0},{9,1},... | collective-permute-start | bytes 1769480 | tf_op jit(solution)/shard_map/ppermute | solution.py:107
  723.0 43.4 %collective-permute-start.47 = (bf16[192,3072]{1,0:T(8,128)(2,1)S(1)}, bf16[192,3072]{1,0:T(8,128)(2,1)S(1)}, u32[]{:S(2)}, u32[]{:S(2)}) collective-permute-start(bf16[192,3072]{1,0:T(8,128)(2,1)S(1)} %slice.494), channel_id=1, source_target_pairs={{0,8},{1,9},{2,10},{3,11},{4,12},{5,13},{6,14},{7,15},{8,0},{9,1},... | collective-permute-start | bytes 3538952 | tf_op jit(solution)/shard_map/ppermute | solution.py:107
  736.5 35.3 %collective-permute-start.54 = (bf16[96,1536]{1,0:T(8,128)(2,1)S(1)}, bf16[96,1536]{1,0:T(8,128)(2,1)S(1)}, u32[]{:S(2)}, u32[]{:S(2)}) collective-permute-start(bf16[96,1536]{1,0:T(8,128)(2,1)S(1)} %slice.506), channel_id=1, source_target_pairs={{0,16},{1,17},{2,18},{3,19},{4,20},{5,21},{6,22},{7,23},{8,24},{9,... | collective-permute-start | bytes 884744 | tf_op jit(solution)/shard_map/ppermute | solution.py:107
  766.8 27.4 %collective-permute-start.48 = (bf16[96,3072]{1,0:T(8,128)(2,1)S(1)}, bf16[96,3072]{1,0:T(8,128)(2,1)S(1)}, u32[]{:S(2)}, u32[]{:S(2)}) collective-permute-start(bf16[96,3072]{1,0:T(8,128)(2,1)S(1)} %slice.501), channel_id=1, source_target_pairs={{0,16},{1,17},{2,18},{3,19},{4,20},{5,21},{6,22},{7,23},{8,24},{9,... | collective-permute-start | bytes 1769480 | tf_op jit(solution)/shard_map/ppermute | solution.py:107
  772.0 23.8 %collective-permute-start.55 = (bf16[48,1536]{1,0:T(8,128)(2,1)S(1)}, bf16[48,1536]{1,0:T(8,128)(2,1)S(1)}, u32[]{:S(2)}, u32[]{:S(2)}) collective-permute-start(bf16[48,1536]{1,0:T(8,128)(2,1)S(1)} %slice.508), channel_id=1, source_target_pairs={{0,4},{1,5},{2,6},{3,7},{4,0},{5,1},{6,2},{7,3},{8,12},{9,13},{10,... | collective-permute-start | bytes 442376 | tf_op jit(solution)/shard_map/ppermute | solution.py:107
  (84 other events, 1525.9 us)
where the time goes:
time: 816 us; the launch traced here: 806 us
  waiting for transfers between devices  386 us (47%)
  matrix products  181 us (22%)
  local copies, waits for them, and re-layouts  104 us (13%)
  starting transfers between devices  59.2 us (7%)
  other arithmetic  43.3 us (5%)
  blocking collectives  29.6 us (4%)
    ppermute x65, waiting for transfers between devices, swap(): return lax.ppermute(array, AXES, [(i, i ^ mask) for i in range(world)])  386 us
    dot_general x16, matrix products, against(): lax.dot_general(left_side, right_side, (((1,), (1,)), ((), ())), preferre...  67.4 us
    dot_general x14, matrix products, product(): return jnp.dot(left_side, right_side, preferred_element_type=f32)  66.6 us
    ppermute x65, starting transfers between devices, swap(): return lax.ppermute(array, AXES, [(i, i ^ mask) for i in range(world)])  59.2 us
    unnamed x201, local copies, waits for them, and re-layouts  42.8 us
    dot_general x14, matrix products, across(): lax.dot_general(left_side, right_side, (((0,), (0,)), ((), ())), preferre...  36.2 us
    psum x1, blocking collectives, per_device(): second = lax.psum(second, 'tensor')  29.6 us
  transfers between devices with their start and end apart: 65, of which 26 were waited for; matrix products, arithmetic and copies ran while one was open for 35% of the time, Pallas kernels for 0%

commit v1 on v0

--- a/solution.py
+++ b/solution.py
@@ -129,6 +129,16 @@
         down_weight,
         cotangent,
     ):
+
+        def part_the_local_data(target, lane_axis):
+            many = lax.psum(1, lane_axis)
+            reached = target
+            for i0 in [
+                [(dev_j, dev_j ^ c) for dev_j in range(many)] for c in (1, 2, 4, 8, 16) if c < many
+            ]:
+                reached = reached + lax.ppermute(reached, lane_axis, i0)
+            return reached
+
         micro, per_pack, width = tokens.shape
         rows = micro * per_pack
         qw, kw = (query_weight.shape[1], key_weight.shape[1])
@@ -308,7 +318,7 @@
         second = jnp.sum(
             gate_weight.astype(f32) * gate_grad + up_weight.astype(f32) * up_grad, axis=1
         )
-        second = lax.psum(second, "tensor")
+        second = part_the_local_data(second, "tensor")
         second = lax.dynamic_slice(second, (t_i * shard,), (shard,))
         second_gain_grad = second / second_gain.astype(f32)
         return (

time: 816 us -> 814 us (level)
  waiting for transfers between devices: 386 us -> 419 us
  blocking collectives: 29.6 us -> 0 us
    psum x1 -> x0, blocking collectives: 29.6 us -> none  [per_device(): second = lax.psum(second, 'tensor')]
    ppermute x0 -> x2, waiting for transfers between devices: none -> 25.7 us  [part_the_local_data(): reached = reached + lax.ppermute(reached, lane_axis, i0)]
    unnamed x201 -> x197, local copies, waits for them, and re-layouts: 42.8 us -> 43.1 us
  transfers between devices with their start and end apart: 65 -> 67, of which waited for: 26 -> 27; matrix products, arithmetic and copies ran while one was open for 35% -> 34% of each run, Pallas kernels for 0% -> 0%
where the time goes in v1:
time: 814 us; the launch traced here: 803 us
  waiting for transfers between devices  419 us (51%)
  matrix products  179 us (22%)
  local copies, waits for them, and re-layouts  104 us (13%)
  starting transfers between devices  57 us (7%)
  other arithmetic  40.7 us (5%)
    ppermute x65, waiting for transfers between devices, swap(): return lax.ppermute(array, AXES, [(i, i ^ mask) for i in range(world)])  393 us
    dot_general x14, matrix products, product(): return jnp.dot(left_side, right_side, preferred_element_type=f32)  66.6 us
    dot_general x16, matrix products, against(): lax.dot_general(left_side, right_side, (((1,), (1,)), ((), ())), preferre...  65.5 us
    ppermute x65, starting transfers between devices, swap(): return lax.ppermute(array, AXES, [(i, i ^ mask) for i in range(world)])  56.5 us
    unnamed x197, local copies, waits for them, and re-layouts  43.1 us
    dot_general x14, matrix products, across(): lax.dot_general(left_side, right_side, (((0,), (0,)), ((), ())), preferre...  36.2 us
    ppermute x2, waiting for transfers between devices, part_the_local_data(): reached = reached + lax.ppermute(reached, lane_axis, i0)  25.7 us
  transfers between devices with their start and end apart: 67, of which 27 were waited for; matrix products, arithmetic and copies ran while one was open for 34% of the time, Pallas kernels for 0%

profile of v1, /device:TPU:0, one launch (start us, length us, event | category | flops | bytes accessed | tf_op | source)
XLA Modules:
  0.0 803.2 jit_solution(9834053031612072950)
XLA Ops:
  0.7 4.1 collective-permute-start.30
  19.4 3.3 fusion.57
  29.8 8.6 %collective-permute-done.4 = bf16[96,3200]{1,0:T(8,128)(2,1)S(1)} collective-permute-done((bf16[96,3200]{1,0:T(8,128)(2,1)S(1)}, bf16[96,3200]{1,0:T(8,128)(2,1)S(1)}, u32[]{:S(2)}, u32[]{:S(2)}) %collective-permute-start.4) | collective-permute-done | bytes 614432 | tf_op jit(solution)/shard_map/ppermute | solution.py:107
  39.7 27.5 %collective-permute-done.1 = bf16[96,3200]{1,0:T(8,128)(2,1)S(1)} collective-permute-done((bf16[96,3200]{1,0:T(8,128)(2,1)S(1)}, bf16[96,3200]{1,0:T(8,128)(2,1)S(1)}, u32[]{:S(2)}, u32[]{:S(2)}) %collective-permute-start.1) | collective-permute-done | bytes 614432 | tf_op jit(solution)/shard_map/ppermute | solution.py:107
  68.1 4.7 collective-permute-done.2
  76.1 8.4 %collective-permute-done.3 = bf16[96,3200]{1,0:T(8,128)(2,1)S(1)} collective-permute-done((bf16[96,3200]{1,0:T(8,128)(2,1)S(1)}, bf16[96,3200]{1,0:T(8,128)(2,1)S(1)}, u32[]{:S(2)}, u32[]{:S(2)}) %collective-permute-start.3) | collective-permute-done | bytes 614432 | tf_op jit(solution)/shard_map/ppermute | solution.py:107
  88.3 13.0 %collective-permute-done.6 = bf16[96,3200]{1,0:T(8,128)(2,1)S(1)} collective-permute-done((bf16[96,3200]{1,0:T(8,128)(2,1)S(1)}, bf16[96,3200]{1,0:T(8,128)(2,1)S(1)}, u32[]{:S(2)}, u32[]{:S(2)}) %collective-permute-start.6) | collective-permute-done | bytes 614432 | tf_op jit(solution)/shard_map/ppermute | solution.py:107
  102.2 9.9 %collective-permute-done.7 = bf16[96,3200]{1,0:T(8,128)(2,1)S(1)} collective-permute-done((bf16[96,3200]{1,0:T(8,128)(2,1)S(1)}, bf16[96,3200]{1,0:T(8,128)(2,1)S(1)}, u32[]{:S(2)}, u32[]{:S(2)}) %collective-permute-start.7) | collective-permute-done | bytes 614432 | tf_op jit(solution)/shard_map/ppermute | solution.py:107
  119.2 5.5 collective-permute-done.14
  126.7 4.3 collective-permute-done.15
  132.5 3.8 collective-permute-done.16
  141.3 7.3 collective-permute-done.34
  149.2 23.1 %collective-permute-done.23 = bf16[192,2048]{1,0:T(8,128)(2,1)S(1)} collective-permute-done((bf16[192,2048]{1,0:T(8,128)(2,1)}, bf16[192,2048]{1,0:T(8,128)(2,1)S(1)}, u32[]{:S(2)}, u32[]{:S(2)}) %collective-permute-start.23) | collective-permute-done | bytes 786464 | tf_op jit(solution)/shard_map/ppermute | solution.py:107
  180.7 4.3 multiply_convert_fusion.4
  185.1 3.6 fusion.149
  188.7 3.7 fusion.137
  192.4 3.2 fusion.140
  195.6 3.4 fusion.15
  204.0 2.7 copy.165
  208.0 2.9 reshape.243
  210.9 3.7 subtract_convert_fusion.1
  220.7 2.8 fusion.181
  254.0 18.9 %collective-permute-done.36 = bf16[192,1024]{1,0:T(8,128)(2,1)S(1)} collective-permute-done((bf16[192,1024]{1,0:T(8,128)(2,1)S(1)}, bf16[192,1024]{1,0:T(8,128)(2,1)S(1)}, u32[]{:S(2)}, u32[]{:S(2)}) %collective-permute-start.36) | collective-permute-done | bytes 393248 | tf_op jit(solution)/shard_map/ppermute | solution.py:107
  280.1 13.4 %collective-permute-done.28 = bf16[192,2048]{1,0:T(8,128)(2,1)S(1)} collective-permute-done((bf16[192,2048]{1,0:T(8,128)(2,1)}, bf16[192,2048]{1,0:T(8,128)(2,1)S(1)}, u32[]{:S(2)}, u32[]{:S(2)}) %collective-permute-start.28) | collective-permute-done | bytes 786464 | tf_op jit(solution)/shard_map/ppermute | solution.py:107
  295.0 13.2 %collective-permute-done.29 = bf16[192,2048]{1,0:T(8,128)(2,1)S(1)} collective-permute-done((bf16[192,2048]{1,0:T(8,128)(2,1)S(1)}, bf16[192,2048]{1,0:T(8,128)(2,1)S(1)}, u32[]{:S(2)}, u32[]{:S(2)}) %collective-permute-start.29) | collective-permute-done | bytes 786464 | tf_op jit(solution)/shard_map/ppermute | solution.py:107
  314.0 16.8 %fusion.176 = f32[1536,2048]{1,0:T(8,128)} fusion(bf16[1536,2048]{1,0:T(8,128)(2,1)S(1)} %copy-done.66, bf16[384,1536]{1,0:T(8,128)(2,1)S(1)} %collective-permute-done.22, bf16[384,1536]{1,0:T(8,128)(2,1)S(1)} %collective-permute-done.21, bf16[384,1536]{1,0:T(8,128)(2,1)S(1)} %collective-permute-done.20, bf16[384,1536]{1,0:T(8,128)(2,1)S(1)} %fusion.47), kind=kOutput, calls=%fused_computation.319 | convolution fusion | flops 9682550784 | bytes 23592960 | tf_op jit(solution)/shard_map/dot_general | solution.py:55
  330.8 14.9 %multiply_convert_fusion.1 = (bf16[1536,1024]{1,0:T(8,128)(2,1)S(1)}, bf16[1536,1024]{1,0:T(8,128)(2,1)}, bf16[1536,1024]{1,0:T(8,128)(2,1)}) fusion(f32[1536,2048]{1,0:T(8,128)} %fusion.176, bf16[1536,1024]{1,0:T(8,128)(2,1)} %constant_dynamic-update-slice_fusion.31, bf16[384,1536]{1,0:T(8,128)(2,1)} %copy-done.40, bf16[384,1536]{1,0:T(8,128)(2,1)} %copy-done.39, ...), kind=kOutput, calls=%fused_computation.19 | convolution fusion | flops 4875878400 | bytes 29884416 | tf_op jit(solution)/shard_map/dot_general | solution.py:55
  345.8 6.8 fusion.92
  354.5 3.8 fusion.89
  359.8 15.1 %convolution_convert_fusion.1 = bf16[1536,1536]{1,0:T(8,128)(2,1)} fusion(bf16[1536,2048]{1,0:T(8,128)(2,1)} %constant_dynamic-update-slice_fusion.22, bf16[1536,1024]{1,0:T(8,128)(2,1)} %get-tuple-element.19, bf16[1536,1024]{1,0:T(8,128)(2,1)S(1)} %get-tuple-element.18), kind=kOutput, calls=%fused_computation.14 | convolution fusion | flops 9678618624 | bytes 17301504 | tf_op jit(solution)/shard_map/dot_general | solution.py:65
  374.8 3.8 fusion.86
  379.2 7.4 convolution_convert_fusion
  390.2 4.1 convert_add_fusion.3
  395.9 28.0 %collective-permute-done.59 = bf16[768,1024]{1,0:T(8,128)(2,1)} collective-permute-done((bf16[768,1024]{1,0:T(8,128)(2,1)}, bf16[768,1024]{1,0:T(8,128)(2,1)}, u32[]{:S(2)}, u32[]{:S(2)}) %collective-permute-start.59) | collective-permute-done | bytes 1572896 | tf_op jit(solution)/shard_map/ppermute | solution.py:107
  424.0 4.1 convert_add_fusion.4
  429.6 24.9 %collective-permute-done.56 = bf16[768,1024]{1,0:T(8,128)(2,1)S(1)} collective-permute-done((bf16[768,1024]{1,0:T(8,128)(2,1)}, bf16[768,1024]{1,0:T(8,128)(2,1)S(1)}, u32[]{:S(2)}, u32[]{:S(2)}) %collective-permute-start.56) | collective-permute-done | bytes 1572896 | tf_op jit(solution)/shard_map/ppermute | solution.py:107
  454.5 2.8 convert_add_fusion.5
  459.7 3.0 collective-permute-start.61
  462.7 24.7 %collective-permute-done.57 = bf16[384,1024]{1,0:T(8,128)(2,1)S(1)} collective-permute-done((bf16[384,1024]{1,0:T(8,128)(2,1)S(1)}, bf16[384,1024]{1,0:T(8,128)(2,1)S(1)}, u32[]{:S(2)}, u32[]{:S(2)}) %collective-permute-start.57) | collective-permute-done | bytes 786464 | tf_op jit(solution)/shard_map/ppermute | solution.py:107
  492.1 12.7 %collective-permute-done.61 = bf16[192,1024]{1,0:T(8,128)(2,1)S(1)} collective-permute-done((bf16[192,1024]{1,0:T(8,128)(2,1)S(1)}, bf16[192,1024]{1,0:T(8,128)(2,1)S(1)}, u32[]{:S(2)}, u32[]{:S(2)}) %collective-permute-start.61) | collective-permute-done | bytes 393248 | tf_op jit(solution)/shard_map/ppermute | solution.py:107
  504.8 5.2 collective-permute-done.58
  520.1 25.7 %collective-permute-done.63 = f32[192]{0:T(256)S(1)} collective-permute-done((f32[192]{0:T(256)S(1)}, f32[192]{0:T(256)S(1)}, u32[]{:S(2)}, u32[]{:S(2)}) %collective-permute-start.63) | collective-permute-done | bytes 800 | tf_op jit(solution)/shard_map/ppermute | solution.py:139
  551.1 2.8 convolution_convert_fusion.5
  562.1 3.2 fusion.46
  565.3 6.2 reshape.247
  571.5 5.2 copy.140
  576.8 3.8 fusion.102
  598.1 3.3 fusion.178
  601.5 3.2 copy.167
  604.7 3.2 copy.168
  607.9 3.7 subtract_convert_fusion
  613.6 4.1 convert_element_type.310
  625.4 3.1 fusion.68
  628.4 3.1 fusion.66
  631.5 3.1 fusion.64
  634.6 3.1 fusion.62
  643.8 4.4 fusion.5
  648.3 69.7 %collective-permute-done.52 = bf16[384,1536]{1,0:T(8,128)(2,1)S(1)} collective-permute-done((bf16[384,1536]{1,0:T(8,128)(2,1)S(1)}, bf16[384,1536]{1,0:T(8,128)(2,1)S(1)}, u32[]{:S(2)}, u32[]{:S(2)}) %collective-permute-start.52) | collective-permute-done | bytes 1179680 | tf_op jit(solution)/shard_map/ppermute | solution.py:107
  722.0 6.1 fusion.40
  728.0 6.7 collective-permute-done.53
  735.0 29.8 %collective-permute-done.47 = bf16[192,3072]{1,0:T(8,128)(2,1)S(1)} collective-permute-done((bf16[192,3072]{1,0:T(8,128)(2,1)S(1)}, bf16[192,3072]{1,0:T(8,128)(2,1)S(1)}, u32[]{:S(2)}, u32[]{:S(2)}) %collective-permute-start.47) | collective-permute-done | bytes 1179680 | tf_op jit(solution)/shard_map/ppermute | solution.py:107
  765.3 4.6 fusion.49
  771.5 20.1 %collective-permute-done.48 = bf16[96,3072]{1,0:T(8,128)(2,1)S(1)} collective-permute-done((bf16[96,3072]{1,0:T(8,128)(2,1)S(1)}, bf16[96,3072]{1,0:T(8,128)(2,1)S(1)}, u32[]{:S(2)}, u32[]{:S(2)}) %collective-permute-start.48) | collective-permute-done | bytes 589856 | tf_op jit(solution)/shard_map/ppermute | solution.py:107
  794.0 6.8 collective-permute-done.49
  (432 shorter events, 198.5 us)
Async XLA Ops:
  0.7 112.3 %collective-permute-start.30 = (bf16[192,1024]{1,0:T(8,128)(2,1)}, bf16[192,1024]{1,0:T(8,128)(2,1)}, u32[]{:S(2)}, u32[]{:S(2)}) collective-permute-start(bf16[192,1024]{1,0:T(8,128)(2,1)} %bitcast.152), channel_id=1, source_target_pairs={{0,16},{1,17},{2,18},{3,19},{4,20},{5,21},{6,22},{7,23},{8,24},{9,... | collective-permute-start | bytes 1179656 | tf_op jit(solution)/shard_map/ppermute | solution.py:107
  4.8 109.7 %collective-permute-start.31 = (bf16[192,1024]{1,0:T(8,128)(2,1)}, bf16[192,1024]{1,0:T(8,128)(2,1)}, u32[]{:S(2)}, u32[]{:S(2)}) collective-permute-start(bf16[192,1024]{1,0:T(8,128)(2,1)} %bitcast.153), channel_id=1, source_target_pairs={{0,8},{1,9},{2,10},{3,11},{4,12},{5,13},{6,14},{7,15},{8,0},{9,1},... | collective-permute-start | bytes 1179656 | tf_op jit(solution)/shard_map/ppermute | solution.py:107
  9.0 14.8 %collective-permute-start = (bf16[48,3200]{1,0:T(8,128)(2,1)S(1)}, bf16[48,3200]{1,0:T(8,128)(2,1)S(1)}, u32[]{:S(2)}, u32[]{:S(2)}) collective-permute-start(bf16[48,3200]{1,0:T(8,128)(2,1)S(1)} %get-tuple-element.40), channel_id=1, source_target_pairs={{0,4},{1,5},{2,6},{3,7},{4,0},{5,1},{6,2},{7,3},{8,12},{9,13},{10,... | collective-permute-start | bytes 921608 | tf_op jit(solution)/shard_map/ppermute | solution.py:107
  10.5 14.9 %collective-permute-start.10 = (bf16[48,1536]{1,0:T(8,128)(2,1)}, bf16[48,1536]{1,0:T(8,128)(2,1)S(1)}, u32[]{:S(2)}, u32[]{:S(2)}) collective-permute-start(bf16[48,1536]{1,0:T(8,128)(2,1)} %param.18), channel_id=1, source_target_pairs={{0,4},{1,5},{2,6},{3,7},{4,0},{5,1},{6,2},{7,3},{8,12},{9,13},{10,... | collective-permute-start | bytes 442376 | tf_op jit(solution)/shard_map/ppermute | solution.py:107
  23.9 14.5 %collective-permute-start.4 = (bf16[96,3200]{1,0:T(8,128)(2,1)S(1)}, bf16[96,3200]{1,0:T(8,128)(2,1)S(1)}, u32[]{:S(2)}, u32[]{:S(2)}) collective-permute-start(bf16[96,3200]{1,0:T(8,128)(2,1)S(1)} %pad_maximum_fusion.6), channel_id=1, source_target_pairs={{0,2},{1,3},{2,0},{3,1},{4,6},{5,7},{6,4},{7,5},{8,10},{9,11},{10,... | collective-permute-start | bytes 1843208 | tf_op jit(solution)/shard_map/ppermute | solution.py:107
  26.1 90.0 %collective-permute-start.11 = (bf16[96,1536]{1,0:T(8,128)(2,1)}, bf16[96,1536]{1,0:T(8,128)(2,1)S(1)}, u32[]{:S(2)}, u32[]{:S(2)}) collective-permute-start(bf16[96,1536]{1,0:T(8,128)(2,1)} %get-tuple-element.42), channel_id=1, source_target_pairs={{0,16},{1,17},{2,18},{3,19},{4,20},{5,21},{6,22},{7,23},{8,24},{9,... | collective-permute-start | bytes 884744 | tf_op jit(solution)/shard_map/ppermute | solution.py:107
  26.5 40.8 %collective-permute-start.1 = (bf16[96,3200]{1,0:T(8,128)(2,1)S(1)}, bf16[96,3200]{1,0:T(8,128)(2,1)S(1)}, u32[]{:S(2)}, u32[]{:S(2)}) collective-permute-start(bf16[96,3200]{1,0:T(8,128)(2,1)S(1)} %pad_maximum_fusion.6), channel_id=1, source_target_pairs={{0,16},{1,17},{2,18},{3,19},{4,20},{5,21},{6,22},{7,23},{8,24},{9,... | collective-permute-start | bytes 1843208 | tf_op jit(solution)/shard_map/ppermute | solution.py:107
  38.4 34.4 %collective-permute-start.2 = (bf16[96,3200]{1,0:T(8,128)(2,1)S(1)}, bf16[96,3200]{1,0:T(8,128)(2,1)S(1)}, u32[]{:S(2)}, u32[]{:S(2)}) collective-permute-start(bf16[96,3200]{1,0:T(8,128)(2,1)S(1)} %pad_maximum_fusion.6), channel_id=1, source_target_pairs={{0,8},{1,9},{2,10},{3,11},{4,12},{5,13},{6,14},{7,15},{8,0},{9,1},... | collective-permute-start | bytes 1843208 | tf_op jit(solution)/shard_map/ppermute | solution.py:107
  67.2 17.2 %collective-permute-start.3 = (bf16[96,3200]{1,0:T(8,128)(2,1)S(1)}, bf16[96,3200]{1,0:T(8,128)(2,1)S(1)}, u32[]{:S(2)}, u32[]{:S(2)}) collective-permute-start(bf16[96,3200]{1,0:T(8,128)(2,1)S(1)} %collective-permute-done.1), channel_id=1, source_target_pairs={{0,8},{1,9},{2,10},{3,11},{4,12},{5,13},{6,14},{7,15},{8,0},{9,1},... | collective-permute-start | bytes 1843208 | tf_op jit(solution)/shard_map/ppermute | solution.py:107
  72.8 14.1 %collective-permute-start.5 = (bf16[96,3200]{1,0:T(8,128)(2,1)S(1)}, bf16[96,3200]{1,0:T(8,128)(2,1)S(1)}, u32[]{:S(2)}, u32[]{:S(2)}) collective-permute-start(bf16[96,3200]{1,0:T(8,128)(2,1)S(1)} %collective-permute-done.1), channel_id=1, source_target_pairs={{0,2},{1,3},{2,0},{3,1},{4,6},{5,7},{6,4},{7,5},{8,10},{9,11},{10,... | collective-permute-start | bytes 1843208 | tf_op jit(solution)/shard_map/ppermute | solution.py:107
  84.5 16.8 %collective-permute-start.6 = (bf16[96,3200]{1,0:T(8,128)(2,1)S(1)}, bf16[96,3200]{1,0:T(8,128)(2,1)S(1)}, u32[]{:S(2)}, u32[]{:S(2)}) collective-permute-start(bf16[96,3200]{1,0:T(8,128)(2,1)S(1)} %collective-permute-done.2), channel_id=1, source_target_pairs={{0,2},{1,3},{2,0},{3,1},{4,6},{5,7},{6,4},{7,5},{8,10},{9,11},{10,... | collective-permute-start | bytes 1843208 | tf_op jit(solution)/shard_map/ppermute | solution.py:107
  86.9 25.2 %collective-permute-start.7 = (bf16[96,3200]{1,0:T(8,128)(2,1)S(1)}, bf16[96,3200]{1,0:T(8,128)(2,1)S(1)}, u32[]{:S(2)}, u32[]{:S(2)}) collective-permute-start(bf16[96,3200]{1,0:T(8,128)(2,1)S(1)} %collective-permute-done.3), channel_id=1, source_target_pairs={{0,2},{1,3},{2,0},{3,1},{4,6},{5,7},{6,4},{7,5},{8,10},{9,11},{10,... | collective-permute-start | bytes 1843208 | tf_op jit(solution)/shard_map/ppermute | solution.py:107
  101.3 15.7 %collective-permute-start.12 = (bf16[96,1536]{1,0:T(8,128)(2,1)}, bf16[96,1536]{1,0:T(8,128)(2,1)S(1)}, u32[]{:S(2)}, u32[]{:S(2)}) collective-permute-start(bf16[96,1536]{1,0:T(8,128)(2,1)} %get-tuple-element.42), channel_id=1, source_target_pairs={{0,8},{1,9},{2,10},{3,11},{4,12},{5,13},{6,14},{7,15},{8,0},{9,1},... | collective-permute-start | bytes 884744 | tf_op jit(solution)/shard_map/ppermute | solution.py:107
  112.1 65.9 %collective-permute-start.8 = (bf16[384,3200]{1,0:T(8,128)(2,1)}, bf16[384,3200]{1,0:T(8,128)(2,1)}, u32[]{:S(2)}, u32[]{:S(2)}) collective-permute-start(bf16[384,3200]{1,0:T(8,128)(2,1)} %constant_dynamic-update-slice_fusion), channel_id=1, source_target_pairs={{0,1},{1,0},{2,3},{3,2},{4,5},{5,4},{6,7},{7,6},{8,9},{9,8},{10,11... | collective-permute-start | bytes 7372808 | tf_op jit(solution)/shard_map/ppermute | solution.py:107
  113.0 66.1 %collective-permute-start.9 = (bf16[384,3200]{1,0:T(8,128)(2,1)}, bf16[384,3200]{1,0:T(8,128)(2,1)}, u32[]{:S(2)}, u32[]{:S(2)}) collective-permute-start(bf16[384,3200]{1,0:T(8,128)(2,1)} %constant_dynamic-update-slice_fusion.5), channel_id=1, source_target_pairs={{0,1},{1,0},{2,3},{3,2},{4,5},{5,4},{6,7},{7,6},{8,9},{9,8},{10,11... | collective-permute-start | bytes 7372808 | tf_op jit(solution)/shard_map/ppermute | solution.py:107
  114.5 10.2 %collective-permute-start.14 = (bf16[96,1536]{1,0:T(8,128)(2,1)}, bf16[96,1536]{1,0:T(8,128)(2,1)S(1)}, u32[]{:S(2)}, u32[]{:S(2)}) collective-permute-start(bf16[96,1536]{1,0:T(8,128)(2,1)} %get-tuple-element.42), channel_id=1, source_target_pairs={{0,2},{1,3},{2,0},{3,1},{4,6},{5,7},{6,4},{7,5},{8,10},{9,11},{10,... | collective-permute-start | bytes 884744 | tf_op jit(solution)/shard_map/ppermute | solution.py:107
  117.0 14.0 %collective-permute-start.15 = (bf16[96,1536]{1,0:T(8,128)(2,1)S(1)}, bf16[96,1536]{1,0:T(8,128)(2,1)S(1)}, u32[]{:S(2)}, u32[]{:S(2)}) collective-permute-start(bf16[96,1536]{1,0:T(8,128)(2,1)S(1)} %collective-permute-done.11), channel_id=1, source_target_pairs={{0,2},{1,3},{2,0},{3,1},{4,6},{5,7},{6,4},{7,5},{8,10},{9,11},{10,... | collective-permute-start | bytes 884744 | tf_op jit(solution)/shard_map/ppermute | solution.py:107
  124.6 11.7 %collective-permute-start.16 = (bf16[96,1536]{1,0:T(8,128)(2,1)S(1)}, bf16[96,1536]{1,0:T(8,128)(2,1)S(1)}, u32[]{:S(2)}, u32[]{:S(2)}) collective-permute-start(bf16[96,1536]{1,0:T(8,128)(2,1)S(1)} %collective-permute-done.12), channel_id=1, source_target_pairs={{0,2},{1,3},{2,0},{3,1},{4,6},{5,7},{6,4},{7,5},{8,10},{9,11},{10,... | collective-permute-start | bytes 884744 | tf_op jit(solution)/shard_map/ppermute | solution.py:107
  126.0 11.1 %collective-permute-start.32 = (bf16[192,1024]{1,0:T(8,128)(2,1)}, bf16[192,1024]{1,0:T(8,128)(2,1)S(1)}, u32[]{:S(2)}, u32[]{:S(2)}) collective-permute-start(bf16[192,1024]{1,0:T(8,128)(2,1)} %collective-permute-done.30), channel_id=1, source_target_pairs={{0,8},{1,9},{2,10},{3,11},{4,12},{5,13},{6,14},{7,15},{8,0},{9,1},... | collective-permute-start | bytes 1179656 | tf_op jit(solution)/shard_map/ppermute | solution.py:107
  131.0 10.3 %collective-permute-start.33 = (bf16[192,1024]{1,0:T(8,128)(2,1)S(1)}, bf16[192,1024]{1,0:T(8,128)(2,1)S(1)}, u32[]{:S(2)}, u32[]{:S(2)}) collective-permute-start(bf16[192,1024]{1,0:T(8,128)(2,1)S(1)} %bitcast.154), channel_id=1, source_target_pairs={{0,4},{1,5},{2,6},{3,7},{4,0},{5,1},{6,2},{7,3},{8,12},{9,13},{10,... | collective-permute-start | bytes 1179656 | tf_op jit(solution)/shard_map/ppermute | solution.py:107
  136.3 35.9 %collective-permute-start.23 = (bf16[192,2048]{1,0:T(8,128)(2,1)}, bf16[192,2048]{1,0:T(8,128)(2,1)S(1)}, u32[]{:S(2)}, u32[]{:S(2)}) collective-permute-start(bf16[192,2048]{1,0:T(8,128)(2,1)} %get-tuple-element.35), channel_id=1, source_target_pairs={{0,16},{1,17},{2,18},{3,19},{4,20},{5,21},{6,22},{7,23},{8,24},{9,... | collective-permute-start | bytes 2359304 | tf_op jit(solution)/shard_map/ppermute | solution.py:107
  137.1 11.5 %collective-permute-start.34 = (bf16[192,1024]{1,0:T(8,128)(2,1)}, bf16[192,1024]{1,0:T(8,128)(2,1)S(1)}, u32[]{:S(2)}, u32[]{:S(2)}) collective-permute-start(bf16[192,1024]{1,0:T(8,128)(2,1)} %collective-permute-done.30), channel_id=1, source_target_pairs={{0,4},{1,5},{2,6},{3,7},{4,0},{5,1},{6,2},{7,3},{8,12},{9,13},{10,... | collective-permute-start | bytes 1179656 | tf_op jit(solution)/shard_map/ppermute | solution.py:107
  141.3 103.9 %collective-permute-start.24 = (bf16[192,2048]{1,0:T(8,128)(2,1)}, bf16[192,2048]{1,0:T(8,128)(2,1)}, u32[]{:S(2)}, u32[]{:S(2)}) collective-permute-start(bf16[192,2048]{1,0:T(8,128)(2,1)} %get-tuple-element.35), channel_id=1, source_target_pairs={{0,8},{1,9},{2,10},{3,11},{4,12},{5,13},{6,14},{7,15},{8,0},{9,1},... | collective-permute-start | bytes 2359304 | tf_op jit(solution)/shard_map/ppermute | solution.py:107
  148.6 26.1 %collective-permute-start.17 = (bf16[96,1536]{1,0:T(8,128)(2,1)S(1)}, bf16[96,1536]{1,0:T(8,128)(2,1)S(1)}, u32[]{:S(2)}, u32[]{:S(2)}) collective-permute-start(bf16[96,1536]{1,0:T(8,128)(2,1)S(1)} %collective-permute-done.13), channel_id=1, source_target_pairs={{0,2},{1,3},{2,0},{3,1},{4,6},{5,7},{6,4},{7,5},{8,10},{9,11},{10,... | collective-permute-start | bytes 884744 | tf_op jit(solution)/shard_map/ppermute | solution.py:107
  172.3 74.5 %collective-permute-start.26 = (bf16[192,2048]{1,0:T(8,128)(2,1)}, bf16[192,2048]{1,0:T(8,128)(2,1)}, u32[]{:S(2)}, u32[]{:S(2)}) collective-permute-start(bf16[192,2048]{1,0:T(8,128)(2,1)} %get-tuple-element.35), channel_id=1, source_target_pairs={{0,4},{1,5},{2,6},{3,7},{4,0},{5,1},{6,2},{7,3},{8,12},{9,13},{10,... | collective-permute-start | bytes 2359304 | tf_op jit(solution)/shard_map/ppermute | solution.py:107
  174.7 100.4 %collective-permute-start.39 = (bf16[384,1536]{1,0:T(8,128)(2,1)}, bf16[384,1536]{1,0:T(8,128)(2,1)}, u32[]{:S(2)}, u32[]{:S(2)}) collective-permute-start(bf16[384,1536]{1,0:T(8,128)(2,1)} %fusion.57), channel_id=1, source_target_pairs={{0,2},{1,3},{2,0},{3,1},{4,6},{5,7},{6,4},{7,5},{8,10},{9,11},{10,... | collective-permute-start | bytes 3538952 | tf_op jit(solution)/shard_map/ppermute | solution.py:107
  178.0 58.2 %collective-permute-start.18 = (bf16[384,1536]{1,0:T(8,128)(2,1)}, bf16[384,1536]{1,0:T(8,128)(2,1)}, u32[]{:S(2)}, u32[]{:S(2)}) collective-permute-start(bf16[384,1536]{1,0:T(8,128)(2,1)} %constant_dynamic-update-slice_fusion.11), channel_id=1, source_target_pairs={{0,1},{1,0},{2,3},{3,2},{4,5},{5,4},{6,7},{7,6},{8,9},{9,8},{10,11... | collective-permute-start | bytes 3538952 | tf_op jit(solution)/shard_map/ppermute | solution.py:107
  179.1 59.7 %collective-permute-start.19 = (bf16[384,1536]{1,0:T(8,128)(2,1)}, bf16[384,1536]{1,0:T(8,128)(2,1)}, u32[]{:S(2)}, u32[]{:S(2)}) collective-permute-start(bf16[384,1536]{1,0:T(8,128)(2,1)} %constant_dynamic-update-slice_fusion.16), channel_id=1, source_target_pairs={{0,1},{1,0},{2,3},{3,2},{4,5},{5,4},{6,7},{7,6},{8,9},{9,8},{10,11... | collective-permute-start | bytes 3538952 | tf_op jit(solution)/shard_map/ppermute | solution.py:107
  236.2 13.3 %collective-permute-start.35 = (bf16[192,1024]{1,0:T(8,128)(2,1)}, bf16[192,1024]{1,0:T(8,128)(2,1)S(1)}, u32[]{:S(2)}, u32[]{:S(2)}) collective-permute-start(bf16[192,1024]{1,0:T(8,128)(2,1)} %collective-permute-done.31), channel_id=1, source_target_pairs={{0,4},{1,5},{2,6},{3,7},{4,0},{5,1},{6,2},{7,3},{8,12},{9,13},{10,... | collective-permute-start | bytes 1179656 | tf_op jit(solution)/shard_map/ppermute | solution.py:107
  238.8 36.3 %collective-permute-start.25 = (bf16[192,2048]{1,0:T(8,128)(2,1)S(1)}, bf16[192,2048]{1,0:T(8,128)(2,1)S(1)}, u32[]{:S(2)}, u32[]{:S(2)}) collective-permute-start(bf16[192,2048]{1,0:T(8,128)(2,1)S(1)} %copy-done.49), channel_id=1, source_target_pairs={{0,8},{1,9},{2,10},{3,11},{4,12},{5,13},{6,14},{7,15},{8,0},{9,1},... | collective-permute-start | bytes 2359304 | tf_op jit(solution)/shard_map/ppermute | solution.py:107
  245.2 30.5 %collective-permute-start.27 = (bf16[192,2048]{1,0:T(8,128)(2,1)S(1)}, bf16[192,2048]{1,0:T(8,128)(2,1)S(1)}, u32[]{:S(2)}, u32[]{:S(2)}) collective-permute-start(bf16[192,2048]{1,0:T(8,128)(2,1)S(1)} %copy-done.49), channel_id=1, source_target_pairs={{0,4},{1,5},{2,6},{3,7},{4,0},{5,1},{6,2},{7,3},{8,12},{9,13},{10,... | collective-permute-start | bytes 2359304 | tf_op jit(solution)/shard_map/ppermute | solution.py:107
  246.8 26.1 %collective-permute-start.36 = (bf16[192,1024]{1,0:T(8,128)(2,1)S(1)}, bf16[192,1024]{1,0:T(8,128)(2,1)S(1)}, u32[]{:S(2)}, u32[]{:S(2)}) collective-permute-start(bf16[192,1024]{1,0:T(8,128)(2,1)S(1)} %copy-done.60), channel_id=1, source_target_pairs={{0,4},{1,5},{2,6},{3,7},{4,0},{5,1},{6,2},{7,3},{8,12},{9,13},{10,... | collective-permute-start | bytes 1179656 | tf_op jit(solution)/shard_map/ppermute | solution.py:107
  249.5 44.0 %collective-permute-start.20 = (bf16[384,1536]{1,0:T(8,128)(2,1)S(1)}, bf16[384,1536]{1,0:T(8,128)(2,1)S(1)}, u32[]{:S(2)}, u32[]{:S(2)}) collective-permute-start(bf16[384,1536]{1,0:T(8,128)(2,1)S(1)} %fusion.47), channel_id=1, source_target_pairs={{0,2},{1,3},{2,0},{3,1},{4,6},{5,7},{6,4},{7,5},{8,10},{9,11},{10,... | collective-permute-start | bytes 3538952 | tf_op jit(solution)/shard_map/ppermute | solution.py:107
  272.9 20.7 %collective-permute-start.28 = (bf16[192,2048]{1,0:T(8,128)(2,1)}, bf16[192,2048]{1,0:T(8,128)(2,1)S(1)}, u32[]{:S(2)}, u32[]{:S(2)}) collective-permute-start(bf16[192,2048]{1,0:T(8,128)(2,1)} %collective-permute-done.24), channel_id=1, source_target_pairs={{0,4},{1,5},{2,6},{3,7},{4,0},{5,1},{6,2},{7,3},{8,12},{9,13},{10,... | collective-permute-start | bytes 2359304 | tf_op jit(solution)/shard_map/ppermute | solution.py:107
  275.1 34.1 %collective-permute-start.40 = (bf16[384,1536]{1,0:T(8,128)(2,1)}, bf16[384,1536]{1,0:T(8,128)(2,1)S(1)}, u32[]{:S(2)}, u32[]{:S(2)}) collective-permute-start(bf16[384,1536]{1,0:T(8,128)(2,1)} %fusion.57), channel_id=1, source_target_pairs={{0,1},{1,0},{2,3},{3,2},{4,5},{5,4},{6,7},{7,6},{8,9},{9,8},{10,11... | collective-permute-start | bytes 3538952 | tf_op jit(solution)/shard_map/ppermute | solution.py:107
  275.1 34.1 %collective-permute-start.41 = (bf16[384,1536]{1,0:T(8,128)(2,1)}, bf16[384,1536]{1,0:T(8,128)(2,1)S(1)}, u32[]{:S(2)}, u32[]{:S(2)}) collective-permute-start(bf16[384,1536]{1,0:T(8,128)(2,1)} %collective-permute-done.39), channel_id=1, source_target_pairs={{0,1},{1,0},{2,3},{3,2},{4,5},{5,4},{6,7},{7,6},{8,9},{9,8},{10,11... | collective-permute-start | bytes 3538952 | tf_op jit(solution)/shard_map/ppermute | solution.py:107
  275.6 32.6 %collective-permute-start.29 = (bf16[192,2048]{1,0:T(8,128)(2,1)S(1)}, bf16[192,2048]{1,0:T(8,128)(2,1)S(1)}, u32[]{:S(2)}, u32[]{:S(2)}) collective-permute-start(bf16[192,2048]{1,0:T(8,128)(2,1)S(1)} %collective-permute-done.25), channel_id=1, source_target_pairs={{0,4},{1,5},{2,6},{3,7},{4,0},{5,1},{6,2},{7,3},{8,12},{9,13},{10,... | collective-permute-start | bytes 2359304 | tf_op jit(solution)/shard_map/ppermute | solution.py:107
  293.5 18.4 %collective-permute-start.21 = (bf16[384,1536]{1,0:T(8,128)(2,1)S(1)}, bf16[384,1536]{1,0:T(8,128)(2,1)S(1)}, u32[]{:S(2)}, u32[]{:S(2)}) collective-permute-start(bf16[384,1536]{1,0:T(8,128)(2,1)S(1)} %fusion.47), channel_id=1, source_target_pairs={{0,1},{1,0},{2,3},{3,2},{4,5},{5,4},{6,7},{7,6},{8,9},{9,8},{10,11... | collective-permute-start | bytes 3538952 | tf_op jit(solution)/shard_map/ppermute | solution.py:107
  293.6 18.4 %collective-permute-start.22 = (bf16[384,1536]{1,0:T(8,128)(2,1)S(1)}, bf16[384,1536]{1,0:T(8,128)(2,1)S(1)}, u32[]{:S(2)}, u32[]{:S(2)}) collective-permute-start(bf16[384,1536]{1,0:T(8,128)(2,1)S(1)} %collective-permute-done.20), channel_id=1, source_target_pairs={{0,1},{1,0},{2,3},{3,2},{4,5},{5,4},{6,7},{7,6},{8,9},{9,8},{10,11... | collective-permute-start | bytes 3538952 | tf_op jit(solution)/shard_map/ppermute | solution.py:107
  352.6 37.7 %collective-permute-start.64 = (bf16[768,1024]{1,0:T(8,128)(2,1)}, bf16[768,1024]{1,0:T(8,128)(2,1)}, u32[]{:S(2)}, u32[]{:S(2)}) collective-permute-start(bf16[768,1024]{1,0:T(8,128)(2,1)} %fusion.92), channel_id=1, source_target_pairs={{0,4},{1,5},{2,6},{3,7},{4,0},{5,1},{6,2},{7,3},{8,12},{9,13},{10,... | collective-permute-start | bytes 4718600 | tf_op jit(solution)/shard_map/ppermute | solution.py:107
  358.3 65.7 %collective-permute-start.59 = (bf16[768,1024]{1,0:T(8,128)(2,1)}, bf16[768,1024]{1,0:T(8,128)(2,1)}, u32[]{:S(2)}, u32[]{:S(2)}) collective-permute-start(bf16[768,1024]{1,0:T(8,128)(2,1)} %fusion.89), channel_id=1, source_target_pairs={{0,4},{1,5},{2,6},{3,7},{4,0},{5,1},{6,2},{7,3},{8,12},{9,13},{10,... | collective-permute-start | bytes 4718600 | tf_op jit(solution)/shard_map/ppermute | solution.py:107
  378.6 75.8 %collective-permute-start.56 = (bf16[768,1024]{1,0:T(8,128)(2,1)}, bf16[768,1024]{1,0:T(8,128)(2,1)S(1)}, u32[]{:S(2)}, u32[]{:S(2)}) collective-permute-start(bf16[768,1024]{1,0:T(8,128)(2,1)} %fusion.86), channel_id=1, source_target_pairs={{0,4},{1,5},{2,6},{3,7},{4,0},{5,1},{6,2},{7,3},{8,12},{9,13},{10,... | collective-permute-start | bytes 4718600 | tf_op jit(solution)/shard_map/ppermute | solution.py:107
  386.8 101.2 %collective-permute-start.42 = (bf16[768,1536]{1,0:T(8,128)(2,1)S(1)}, bf16[768,1536]{1,0:T(8,128)(2,1)}, u32[]{:S(2)}, u32[]{:S(2)}) collective-permute-start(bf16[768,1536]{1,0:T(8,128)(2,1)S(1)} %slice.327), channel_id=1, source_target_pairs={{0,1},{1,0},{2,3},{3,2},{4,5},{5,4},{6,7},{7,6},{8,9},{9,8},{10,11... | collective-permute-start | bytes 7077896 | tf_op jit(solution)/shard_map/ppermute | solution.py:107
  388.5 122.9 %collective-permute-start.37 = (bf16[768,1536]{1,0:T(8,128)(2,1)}, bf16[768,1536]{1,0:T(8,128)(2,1)}, u32[]{:S(2)}, u32[]{:S(2)}) collective-permute-start(bf16[768,1536]{1,0:T(8,128)(2,1)} %slice.323), channel_id=1, source_target_pairs={{0,1},{1,0},{2,3},{3,2},{4,5},{5,4},{6,7},{7,6},{8,9},{9,8},{10,11... | collective-permute-start | bytes 7077896 | tf_op jit(solution)/shard_map/ppermute | solution.py:107
  394.5 64.5 %collective-permute-start.65 = (bf16[384,1024]{1,0:T(8,128)(2,1)S(1)}, bf16[384,1024]{1,0:T(8,128)(2,1)S(1)}, u32[]{:S(2)}, u32[]{:S(2)}) collective-permute-start(bf16[384,1024]{1,0:T(8,128)(2,1)S(1)} %slice.497), channel_id=1, source_target_pairs={{0,8},{1,9},{2,10},{3,11},{4,12},{5,13},{6,14},{7,15},{8,0},{9,1},... | collective-permute-start | bytes 2359304 | tf_op jit(solution)/shard_map/ppermute | solution.py:107
  428.2 31.2 %collective-permute-start.60 = (bf16[384,1024]{1,0:T(8,128)(2,1)S(1)}, bf16[384,1024]{1,0:T(8,128)(2,1)S(1)}, u32[]{:S(2)}, u32[]{:S(2)}) collective-permute-start(bf16[384,1024]{1,0:T(8,128)(2,1)S(1)} %slice.498), channel_id=1, source_target_pairs={{0,8},{1,9},{2,10},{3,11},{4,12},{5,13},{6,14},{7,15},{8,0},{9,1},... | collective-permute-start | bytes 2359304 | tf_op jit(solution)/shard_map/ppermute | solution.py:107
  457.4 30.1 %collective-permute-start.57 = (bf16[384,1024]{1,0:T(8,128)(2,1)S(1)}, bf16[384,1024]{1,0:T(8,128)(2,1)S(1)}, u32[]{:S(2)}, u32[]{:S(2)}) collective-permute-start(bf16[384,1024]{1,0:T(8,128)(2,1)S(1)} %slice.499), channel_id=1, source_target_pairs={{0,8},{1,9},{2,10},{3,11},{4,12},{5,13},{6,14},{7,15},{8,0},{9,1},... | collective-permute-start | bytes 2359304 | tf_op jit(solution)/shard_map/ppermute | solution.py:107
  459.4 59.7 %collective-permute-start.66 = (bf16[192,1024]{1,0:T(8,128)(2,1)S(1)}, bf16[192,1024]{1,0:T(8,128)(2,1)S(1)}, u32[]{:S(2)}, u32[]{:S(2)}) collective-permute-start(bf16[192,1024]{1,0:T(8,128)(2,1)S(1)} %slice.503), channel_id=1, source_target_pairs={{0,16},{1,17},{2,18},{3,19},{4,20},{5,21},{6,22},{7,23},{8,24},{9,... | collective-permute-start | bytes 1179656 | tf_op jit(solution)/shard_map/ppermute | solution.py:107
  459.7 45.0 %collective-permute-start.61 = (bf16[192,1024]{1,0:T(8,128)(2,1)S(1)}, bf16[192,1024]{1,0:T(8,128)(2,1)S(1)}, u32[]{:S(2)}, u32[]{:S(2)}) collective-permute-start(bf16[192,1024]{1,0:T(8,128)(2,1)S(1)} %slice.504), channel_id=1, source_target_pairs={{0,16},{1,17},{2,18},{3,19},{4,20},{5,21},{6,22},{7,23},{8,24},{9,... | collective-permute-start | bytes 1179656 | tf_op jit(solution)/shard_map/ppermute | solution.py:107
  487.7 22.2 %collective-permute-start.58 = (bf16[192,1024]{1,0:T(8,128)(2,1)S(1)}, bf16[192,1024]{1,0:T(8,128)(2,1)S(1)}, u32[]{:S(2)}, u32[]{:S(2)}) collective-permute-start(bf16[192,1024]{1,0:T(8,128)(2,1)S(1)} %slice.505), channel_id=1, source_target_pairs={{0,16},{1,17},{2,18},{3,19},{4,20},{5,21},{6,22},{7,23},{8,24},{9,... | collective-permute-start | bytes 1179656 | tf_op jit(solution)/shard_map/ppermute | solution.py:107
  490.5 55.9 %collective-permute-start.43 = (bf16[384,1536]{1,0:T(8,128)(2,1)S(1)}, bf16[384,1536]{1,0:T(8,128)(2,1)S(1)}, u32[]{:S(2)}, u32[]{:S(2)}) collective-permute-start(bf16[384,1536]{1,0:T(8,128)(2,1)S(1)} %slice.495), channel_id=1, source_target_pairs={{0,2},{1,3},{2,0},{3,1},{4,6},{5,7},{6,4},{7,5},{8,10},{9,11},{10,... | collective-permute-start | bytes 3538952 | tf_op jit(solution)/shard_map/ppermute | solution.py:107
  517.1 248.2 %collective-permute-start.38 = (bf16[384,1536]{1,0:T(8,128)(2,1)}, bf16[384,1536]{1,0:T(8,128)(2,1)}, u32[]{:S(2)}, u32[]{:S(2)}) collective-permute-start(bf16[384,1536]{1,0:T(8,128)(2,1)} %slice.496), channel_id=1, source_target_pairs={{0,2},{1,3},{2,0},{3,1},{4,6},{5,7},{6,4},{7,5},{8,10},{9,11},{10,... | collective-permute-start | bytes 3538952 | tf_op jit(solution)/shard_map/ppermute | solution.py:107
  518.6 27.2 %collective-permute-start.63 = (f32[192]{0:T(256)S(1)}, f32[192]{0:T(256)S(1)}, u32[]{:S(2)}, u32[]{:S(2)}) collective-permute-start(f32[192]{0:T(256)S(1)} %add.303), channel_id=1, source_target_pairs={{0,2},{1,3},{2,0},{3,1},{4,6},{5,7},{6,4},{7,5},{8,10},{9,11},{10,... | collective-permute-start | bytes 2312 | tf_op jit(solution)/shard_map/ppermute | solution.py:139
  621.1 16.6 %collective-permute-start.45 = (bf16[384,3072]{1,0:T(8,128)(2,1)S(1)}, bf16[384,3072]{1,0:T(8,128)(2,1)S(1)}, u32[]{:S(2)}, u32[]{:S(2)}) collective-permute-start(bf16[384,3072]{1,0:T(8,128)(2,1)S(1)} %convolution_convert_fusion.2), channel_id=1, source_target_pairs={{0,1},{1,0},{2,3},{3,2},{4,5},{5,4},{6,7},{7,6},{8,9},{9,8},{10,11... | collective-permute-start | bytes 7077896 | tf_op jit(solution)/shard_map/ppermute | solution.py:107
  622.4 25.9 %collective-permute-start.50 = (bf16[384,1536]{1,0:T(8,128)(2,1)S(1)}, bf16[384,1536]{1,0:T(8,128)(2,1)S(1)}, u32[]{:S(2)}, u32[]{:S(2)}) collective-permute-start(bf16[384,1536]{1,0:T(8,128)(2,1)S(1)} %copy-done.45), channel_id=1, source_target_pairs={{0,1},{1,0},{2,3},{3,2},{4,5},{5,4},{6,7},{7,6},{8,9},{9,8},{10,11... | collective-permute-start | bytes 3538952 | tf_op jit(solution)/shard_map/ppermute | solution.py:107
  622.6 18.4 %collective-permute-start.51 = (bf16[384,1536]{1,0:T(8,128)(2,1)S(1)}, bf16[384,1536]{1,0:T(8,128)(2,1)S(1)}, u32[]{:S(2)}, u32[]{:S(2)}) collective-permute-start(bf16[384,1536]{1,0:T(8,128)(2,1)S(1)} %convolution_convert_fusion.4), channel_id=1, source_target_pairs={{0,1},{1,0},{2,3},{3,2},{4,5},{5,4},{6,7},{7,6},{8,9},{9,8},{10,11... | collective-permute-start | bytes 3538952 | tf_op jit(solution)/shard_map/ppermute | solution.py:107
  624.3 94.2 %collective-permute-start.44 = (bf16[384,3072]{1,0:T(8,128)(2,1)S(1)}, bf16[384,3072]{1,0:T(8,128)(2,1)S(1)}, u32[]{:S(2)}, u32[]{:S(2)}) collective-permute-start(bf16[384,3072]{1,0:T(8,128)(2,1)S(1)} %convolution_convert_fusion.3), channel_id=1, source_target_pairs={{0,1},{1,0},{2,3},{3,2},{4,5},{5,4},{6,7},{7,6},{8,9},{9,8},{10,11... | collective-permute-start | bytes 7077896 | tf_op jit(solution)/shard_map/ppermute | solution.py:107
  639.1 79.4 %collective-permute-start.46 = (bf16[384,3072]{1,0:T(8,128)(2,1)S(1)}, bf16[384,3072]{1,0:T(8,128)(2,1)S(1)}, u32[]{:S(2)}, u32[]{:S(2)}) collective-permute-start(bf16[384,3072]{1,0:T(8,128)(2,1)S(1)} %add_convert_fusion), channel_id=1, source_target_pairs={{0,2},{1,3},{2,0},{3,1},{4,6},{5,7},{6,4},{7,5},{8,10},{9,11},{10,... | collective-permute-start | bytes 7077896 | tf_op jit(solution)/shard_map/ppermute | solution.py:107
  641.8 76.1 %collective-permute-start.52 = (bf16[384,1536]{1,0:T(8,128)(2,1)S(1)}, bf16[384,1536]{1,0:T(8,128)(2,1)S(1)}, u32[]{:S(2)}, u32[]{:S(2)}) collective-permute-start(bf16[384,1536]{1,0:T(8,128)(2,1)S(1)} %add_convert_fusion.3), channel_id=1, source_target_pairs={{0,2},{1,3},{2,0},{3,1},{4,6},{5,7},{6,4},{7,5},{8,10},{9,11},{10,... | collective-permute-start | bytes 3538952 | tf_op jit(solution)/shard_map/ppermute | solution.py:107
  718.4 16.3 %collective-permute-start.53 = (bf16[192,1536]{1,0:T(8,128)(2,1)S(1)}, bf16[192,1536]{1,0:T(8,128)(2,1)S(1)}, u32[]{:S(2)}, u32[]{:S(2)}) collective-permute-start(bf16[192,1536]{1,0:T(8,128)(2,1)S(1)} %slice.500), channel_id=1, source_target_pairs={{0,8},{1,9},{2,10},{3,11},{4,12},{5,13},{6,14},{7,15},{8,0},{9,1},... | collective-permute-start | bytes 1769480 | tf_op jit(solution)/shard_map/ppermute | solution.py:107
  719.9 44.9 %collective-permute-start.47 = (bf16[192,3072]{1,0:T(8,128)(2,1)S(1)}, bf16[192,3072]{1,0:T(8,128)(2,1)S(1)}, u32[]{:S(2)}, u32[]{:S(2)}) collective-permute-start(bf16[192,3072]{1,0:T(8,128)(2,1)S(1)} %slice.494), channel_id=1, source_target_pairs={{0,8},{1,9},{2,10},{3,11},{4,12},{5,13},{6,14},{7,15},{8,0},{9,1},... | collective-permute-start | bytes 3538952 | tf_op jit(solution)/shard_map/ppermute | solution.py:107
  734.9 34.9 %collective-permute-start.54 = (bf16[96,1536]{1,0:T(8,128)(2,1)S(1)}, bf16[96,1536]{1,0:T(8,128)(2,1)S(1)}, u32[]{:S(2)}, u32[]{:S(2)}) collective-permute-start(bf16[96,1536]{1,0:T(8,128)(2,1)S(1)} %slice.506), channel_id=1, source_target_pairs={{0,16},{1,17},{2,18},{3,19},{4,20},{5,21},{6,22},{7,23},{8,24},{9,... | collective-permute-start | bytes 884744 | tf_op jit(solution)/shard_map/ppermute | solution.py:107
  765.2 26.4 %collective-permute-start.48 = (bf16[96,3072]{1,0:T(8,128)(2,1)S(1)}, bf16[96,3072]{1,0:T(8,128)(2,1)S(1)}, u32[]{:S(2)}, u32[]{:S(2)}) collective-permute-start(bf16[96,3072]{1,0:T(8,128)(2,1)S(1)} %slice.501), channel_id=1, source_target_pairs={{0,16},{1,17},{2,18},{3,19},{4,20},{5,21},{6,22},{7,23},{8,24},{9,... | collective-permute-start | bytes 1769480 | tf_op jit(solution)/shard_map/ppermute | solution.py:107
  770.0 23.2 %collective-permute-start.55 = (bf16[48,1536]{1,0:T(8,128)(2,1)S(1)}, bf16[48,1536]{1,0:T(8,128)(2,1)S(1)}, u32[]{:S(2)}, u32[]{:S(2)}) collective-permute-start(bf16[48,1536]{1,0:T(8,128)(2,1)S(1)} %slice.508), channel_id=1, source_target_pairs={{0,4},{1,5},{2,6},{3,7},{4,0},{5,1},{6,2},{7,3},{8,12},{9,13},{10,... | collective-permute-start | bytes 442376 | tf_op jit(solution)/shard_map/ppermute | solution.py:107
  (84 other events, 1552.8 us)
